TPU v7x, 512 devices: a whole 4x8x8 slice. The times are simulated.
512 devices in a mesh: state: 16 (over y_lo, x), space: 32 (over z, y_hi, core).
Axes of the slice: x: 4, y: 8 (y_hi: 2, y_lo: 4; y = y_hi * 4 + y_lo), z: 8, core: 2. Of those that a mesh axis runs over, the one named last changes fastest.
Arguments:
- states_in: bfloat16 [1536, 32768], P('state', 'space'), may hold values from -12 to 12
- cell_matrices: bfloat16 [64, 512, 512], P('space'), may hold values from -0.5 to 1.5, as said below
- connectivity: int32 [64, 512], P('space'), may hold values from 0 to 32767, as said below
- potential: float32 [32768], P('space'), may hold values from 0.2 to 1.2
Outputs:
- filtered: bfloat16 [1536, 32768], P('state', 'space')
- intersection: float32 [1536, 1536], P('state', 'space')
- projected: float32 [1536, 1536], P('state', 'space')
Inputs may be any that keep to these rules, and one draw needn't show every extreme that they name: `cell_matrices`: each cell's matrix is symmetric. `connectivity`: the cells of rows s * 2 to (s + 1) * 2 - 1 name only nodes from s * 1024 - 128 to (s + 1) * 1024 + 127. A node may be named by several cells, or twice in one cell, or by none.
All inputs are finite; a program needn't handle non-finite values.
Results may differ from a plain program's by a relative error of at most 0.019.
Values may be sent and summed in bfloat16 or wider, within the bound.
A program may use at most 64 MiB of HBM per device.

v0:
```python
import jax
import jax.numpy as jnp
from jax import lax
from jax.sharding import Mesh
from jax.sharding import PartitionSpec as P

DEGREE = 4
STATE = ("state_0", "state_1")


spectrum_center = 3.0
spectrum_half = 3.5


def padded(shard, sides, width):
    for axis, dim in sides:
        size, length = (lax.axis_size(axis), shard.shape[dim])
        up = [(i, (i + 1) % size) for i in range(size - 1)]
        down = [(j, i) for i, j in up]
        last = lax.slice_in_dim(shard, length - width, length, axis=dim)
        leading = lax.slice_in_dim(shard, 0, width, axis=dim)
        before = lax.ppermute(last, axis, up)
        after = lax.ppermute(leading, axis, down)
        shard = jnp.concatenate([before, shard, after], axis=dim)
    return shard


def shifted(block, axis, distance):
    devices = range(lax.axis_size(axis))
    route = [(i - distance, i) for i in devices if i - distance in devices]
    return lax.ppermute(block, axis, route)


def joined_along(pieces, dim):
    shape = list(pieces.shape[1:])
    shape[dim] *= pieces.shape[0]
    return jnp.moveaxis(pieces, 0, dim).reshape(shape)


def gather_in_order(shard, axes, turns):
    pieces = shard[None]
    for k in turns:
        pieces = lax.all_gather(pieces, axes[k], axis=0, tiled=True)
    carried = [lax.axis_size(axes[k]) for k in reversed(turns)]
    pieces = pieces.reshape(*carried, *shard.shape)
    turned = sorted(range(len(turns)), key=lambda place: turns[len(turns) - 1 - place])
    return pieces.transpose(*turned, *range(len(turns), pieces.ndim)).reshape(-1, *shard.shape)


def gathered_by_axis(shard, axes, turns, dim):
    return joined_along(gather_in_order(shard, axes, turns), dim)


def split_up(shard, dim, length):
    shape = shard.shape
    pieces = shard.reshape(*shape[:dim], length, shape[dim] // length, *shape[dim + 1 :])
    return jnp.moveaxis(pieces, dim, 0)


def summed_on_arrival(shard, axis, dim):
    length = lax.axis_size(axis)
    pieces = lax.all_to_all(split_up(shard, dim, length), axis, 0, 0, tiled=True)
    return jnp.sum(pieces.astype(jnp.float32), axis=0)


def in_one_piece(arrays, axis, dim, along):
    both = jnp.concatenate(arrays, axis=along)
    filled, at, done = (summed_on_arrival(both, axis, dim), 0, [])
    for a in arrays:
        done.append(lax.slice_in_dim(filled, at, at + a.shape[along], axis=along))
        at += a.shape[along]
    return tuple(done)


def apply_hamiltonian(states, cell_matrices, local_index, potential, rim_width):
    node_count = states.shape[1]
    extended = padded(states, (("space", 1),), rim_width)
    picked = extended[:, local_index]
    products = jnp.einsum("scp,cpq->scq", picked, cell_matrices, preferred_element_type=jnp.float32)
    summed = jnp.zeros(extended.shape, jnp.float32)
    summed = summed.at[:, local_index.reshape(-1)].add(products.reshape(states.shape[0], -1))
    owned = summed[:, rim_width : rim_width + node_count]
    from_upper = shifted(summed[:, :rim_width], "space", -1)
    from_lower = shifted(summed[:, rim_width + node_count :], "space", 1)
    owned = owned.at[:, node_count - rim_width :].add(from_upper)
    owned = owned.at[:, :rim_width].add(from_lower)
    return owned + potential[None, :] * states.astype(jnp.float32)


def per_device(states_in, cell_matrices, connectivity, potential):
    node_count = states_in.shape[1]
    rim_width = cell_matrices.shape[1] // 4
    offset = lax.axis_index("space") * node_count - rim_width
    local_index = connectivity - offset
    earlier = states_in
    first = (
        apply_hamiltonian(earlier, cell_matrices, local_index, potential, rim_width)
        - spectrum_center * earlier.astype(jnp.float32)
    ) / spectrum_half
    current = first.astype(jnp.bfloat16)
    for section_index in range(DEGREE - 1):
        image = apply_hamiltonian(current, cell_matrices, local_index, potential, rim_width)
        following = 2.0 * (
            image - spectrum_center * current.astype(jnp.float32)
        ) / spectrum_half - earlier.astype(jnp.float32)
        earlier = current
        current = following.astype(jnp.bfloat16)
    total_nodes = node_count * lax.axis_size("space")
    contract = (((1,), (1,)), ((), ()))
    gathered = gathered_by_axis(current, STATE, (0, 1), 0)
    energy = apply_hamiltonian(current, cell_matrices, local_index, potential, rim_width)
    intersection = lax.dot_general(current, gathered, contract, preferred_element_type=jnp.float32)
    projected = lax.dot_general(energy, gathered.astype(jnp.float32), contract)
    intersection = intersection / total_nodes
    projected = projected / total_nodes
    intersection, projected = in_one_piece(
        (intersection.astype(jnp.bfloat16), projected.astype(jnp.bfloat16)), "space", 1, 0
    )
    return (current, intersection, projected)


def solution(mesh):
    finer = Mesh(mesh.devices.reshape(4, 4, mesh.shape["space"]), ("state_0", "state_1", "space"))
    placed = (P(STATE, "space"), P("space", None, None), P("space", None), P("space"))
    return jax.shard_map(
        per_device,
        mesh=finer,
        in_specs=placed,
        out_specs=(P(STATE, "space"), P(STATE, "space"), P(STATE, "space")),
        check_vma=False,
    )
```

profile of v0, /device:TPU:8, one launch (start us, length us, event | category | flops | bytes accessed | tf_op | source)
XLA Modules:
  0.0 309.3 jit_solution(13554139094335774050)
XLA Ops:
  7.2 1.2 copy.62
  8.4 1.7 collective-permute-start
  10.2 1.3 collective-permute-start.1
  11.5 0.7 fusion.47
  12.2 5.8 %collective-permute-done.1 = bf16[96,128]{0,1:T(8,128)(2,1)S(1)} collective-permute-done((bf16[96,128]{0,1:T(8,128)(2,1)S(1)}, bf16[96,128]{0,1:T(8,128)(2,1)S(1)}, u32[]{:S(2)}, u32[]{:S(2)}) %collective-permute-start.1) | collective-permute-done | bytes 24608 | tf_op jit(solution)/shard_map/ppermute | solution.py:23
  18.1 3.2 %gather_fusion = bf16[1024,96]{1,0:T(8,128)(2,1)S(1)} fusion(bf16[96,1280]{0,1:T(8,128)(2,1)S(1)} %pad_maximum_fusion.1, s32[1024]{0:T(1024)S(1)} %broadcast_clamp_fusion), kind=kCustom, calls=%fused_computation | custom fusion | bytes 397312 | tf_op jit(solution)/shard_map/gather | solution.py:78
  22.0 6.2 %scatter_custom_fusion = f32[96,1280]{0,1:T(8,128)S(1)} fusion(s32[1024]{0:T(1024)S(1)} %bitcast.92, f32[1024,96]{1,0:T(8,128)S(1)} %copy.67, f32[]{:T(128)} %constant.238.clone.1), kind=kCustom, calls=%fused_computation.64 | custom fusion | flops 98304 | bytes 491524 | tf_op jit(solution)/shard_map/scatter-add | solution.py:81
  28.2 1.3 collective-permute-start.2
  30.2 9.4 %collective-permute-start.3 = (f32[96,128]{0,1:T(8,128)S(1)}, f32[96,128]{0,1:T(8,128)S(1)}, u32[]{:S(2)}, u32[]{:S(2)}) collective-permute-start(f32[96,128]{0,1:T(8,128)S(1)} %get-tuple-element.143), channel_id=1, source_target_pairs={{0,1},{1,2},{2,3},{3,4},{4,5},{5,6},{6,7},{7,8},{8,9},{9,10},{10,1... | collective-permute-start | bytes 147464 | tf_op jit(solution)/shard_map/ppermute | solution.py:31
  39.6 0.9 collective-permute-done.3
  41.4 8.5 %collective-permute-start.4 = (bf16[96,128]{0,1:T(8,128)(2,1)S(1)}, bf16[96,128]{0,1:T(8,128)(2,1)S(1)}, u32[]{:S(2)}, u32[]{:S(2)}) collective-permute-start(bf16[96,128]{0,1:T(8,128)(2,1)S(1)} %get-tuple-element.151), channel_id=1, source_target_pairs={{0,1},{1,2},{2,3},{3,4},{4,5},{5,6},{6,7},{7,8},{8,9},{9,10},{10,1... | collective-permute-start | bytes 73736 | tf_op jit(solution)/shard_map/ppermute | solution.py:22
  49.9 1.3 collective-permute-start.5
  51.2 7.7 %collective-permute-done.5 = bf16[96,128]{0,1:T(8,128)(2,1)S(1)} collective-permute-done((bf16[96,128]{0,1:T(8,128)(2,1)S(1)}, bf16[96,128]{0,1:T(8,128)(2,1)S(1)}, u32[]{:S(2)}, u32[]{:S(2)}) %collective-permute-start.5) | collective-permute-done | bytes 24608 | tf_op jit(solution)/shard_map/ppermute | solution.py:23
  59.0 3.2 %gather_fusion.1 = bf16[1024,96]{1,0:T(8,128)(2,1)S(1)} fusion(bf16[96,1280]{0,1:T(8,128)(2,1)S(1)} %pad_maximum_fusion.2, s32[1024]{0:T(1024)S(1)} %broadcast_clamp_fusion), kind=kCustom, calls=%fused_computation.1 | custom fusion | bytes 397312 | tf_op jit(solution)/shard_map/gather | solution.py:78
  62.9 6.2 %scatter_custom_fusion.1 = f32[96,1280]{0,1:T(8,128)S(1)} fusion(s32[1024]{0:T(1024)S(1)} %bitcast.93, f32[1024,96]{1,0:T(8,128)S(1)} %copy.71, f32[]{:T(128)} %constant.238.clone.1), kind=kCustom, calls=%fused_computation.62 | custom fusion | flops 98304 | bytes 491524 | tf_op jit(solution)/shard_map/scatter-add | solution.py:81
  69.2 1.3 collective-permute-start.6
  70.5 9.1 %collective-permute-start.7 = (f32[96,128]{0,1:T(8,128)S(1)}, f32[96,128]{0,1:T(8,128)S(1)}, u32[]{:S(2)}, u32[]{:S(2)}) collective-permute-start(f32[96,128]{0,1:T(8,128)S(1)} %get-tuple-element.141), channel_id=1, source_target_pairs={{0,1},{1,2},{2,3},{3,4},{4,5},{5,6},{6,7},{7,8},{8,9},{9,10},{10,1... | collective-permute-start | bytes 147464 | tf_op jit(solution)/shard_map/ppermute | solution.py:31
  79.6 0.9 collective-permute-done.7
  81.4 8.0 %collective-permute-start.8 = (bf16[96,128]{0,1:T(8,128)(2,1)S(1)}, bf16[96,128]{0,1:T(8,128)(2,1)S(1)}, u32[]{:S(2)}, u32[]{:S(2)}) collective-permute-start(bf16[96,128]{0,1:T(8,128)(2,1)S(1)} %get-tuple-element.149), channel_id=1, source_target_pairs={{0,1},{1,2},{2,3},{3,4},{4,5},{5,6},{6,7},{7,8},{8,9},{9,10},{10,1... | collective-permute-start | bytes 73736 | tf_op jit(solution)/shard_map/ppermute | solution.py:22
  89.4 1.3 collective-permute-start.9
  90.7 7.6 %collective-permute-done.9 = bf16[96,128]{0,1:T(8,128)(2,1)S(1)} collective-permute-done((bf16[96,128]{0,1:T(8,128)(2,1)S(1)}, bf16[96,128]{0,1:T(8,128)(2,1)S(1)}, u32[]{:S(2)}, u32[]{:S(2)}) %collective-permute-start.9) | collective-permute-done | bytes 24608 | tf_op jit(solution)/shard_map/ppermute | solution.py:23
  98.4 3.2 %gather_fusion.2 = bf16[1024,96]{1,0:T(8,128)(2,1)S(1)} fusion(bf16[96,1280]{0,1:T(8,128)(2,1)S(1)} %pad_maximum_fusion.3, s32[1024]{0:T(1024)S(1)} %broadcast_clamp_fusion), kind=kCustom, calls=%fused_computation.2 | custom fusion | bytes 397312 | tf_op jit(solution)/shard_map/gather | solution.py:78
  102.3 6.2 %scatter_custom_fusion.2 = f32[96,1280]{0,1:T(8,128)S(1)} fusion(s32[1024]{0:T(1024)S(1)} %bitcast.94, f32[1024,96]{1,0:T(8,128)S(1)} %copy.74, f32[]{:T(128)} %constant.238.clone.1), kind=kCustom, calls=%fused_computation.60 | custom fusion | flops 98304 | bytes 491524 | tf_op jit(solution)/shard_map/scatter-add | solution.py:81
  108.5 1.3 collective-permute-start.10
  109.8 9.1 %collective-permute-start.11 = (f32[96,128]{0,1:T(8,128)S(1)}, f32[96,128]{0,1:T(8,128)S(1)}, u32[]{:S(2)}, u32[]{:S(2)}) collective-permute-start(f32[96,128]{0,1:T(8,128)S(1)} %get-tuple-element.139), channel_id=1, source_target_pairs={{0,1},{1,2},{2,3},{3,4},{4,5},{5,6},{6,7},{7,8},{8,9},{9,10},{10,1... | collective-permute-start | bytes 147464 | tf_op jit(solution)/shard_map/ppermute | solution.py:31
  118.9 0.9 collective-permute-done.11
  120.7 8.0 %collective-permute-start.12 = (bf16[96,128]{0,1:T(8,128)(2,1)S(1)}, bf16[96,128]{0,1:T(8,128)(2,1)S(1)}, u32[]{:S(2)}, u32[]{:S(2)}) collective-permute-start(bf16[96,128]{0,1:T(8,128)(2,1)S(1)} %get-tuple-element.147), channel_id=1, source_target_pairs={{0,1},{1,2},{2,3},{3,4},{4,5},{5,6},{6,7},{7,8},{8,9},{9,10},{10,1... | collective-permute-start | bytes 73736 | tf_op jit(solution)/shard_map/ppermute | solution.py:22
  128.7 1.5 collective-permute-start.13
  130.2 7.4 %collective-permute-done.13 = bf16[96,128]{0,1:T(8,128)(2,1)S(1)} collective-permute-done((bf16[96,128]{0,1:T(8,128)(2,1)S(1)}, bf16[96,128]{0,1:T(8,128)(2,1)S(1)}, u32[]{:S(2)}, u32[]{:S(2)}) %collective-permute-start.13) | collective-permute-done | bytes 24608 | tf_op jit(solution)/shard_map/ppermute | solution.py:23
  137.7 3.2 %gather_fusion.3 = bf16[1024,96]{1,0:T(8,128)(2,1)S(1)} fusion(bf16[96,1280]{0,1:T(8,128)(2,1)S(1)} %pad_maximum_fusion.4, s32[1024]{0:T(1024)S(1)} %broadcast_clamp_fusion), kind=kCustom, calls=%fused_computation.3 | custom fusion | bytes 397312 | tf_op jit(solution)/shard_map/gather | solution.py:78
  141.6 6.2 %scatter_custom_fusion.3 = f32[96,1280]{0,1:T(8,128)S(1)} fusion(s32[1024]{0:T(1024)S(1)} %bitcast.95, f32[1024,96]{1,0:T(8,128)S(1)} %copy.77, f32[]{:T(128)} %constant.238.clone.1), kind=kCustom, calls=%fused_computation.58 | custom fusion | flops 98304 | bytes 491524 | tf_op jit(solution)/shard_map/scatter-add | solution.py:81
  147.8 1.3 collective-permute-start.14
  149.1 9.1 %collective-permute-start.15 = (f32[96,128]{0,1:T(8,128)S(1)}, f32[96,128]{0,1:T(8,128)S(1)}, u32[]{:S(2)}, u32[]{:S(2)}) collective-permute-start(f32[96,128]{0,1:T(8,128)S(1)} %get-tuple-element.137), channel_id=1, source_target_pairs={{0,1},{1,2},{2,3},{3,4},{4,5},{5,6},{6,7},{7,8},{8,9},{9,10},{10,1... | collective-permute-start | bytes 147464 | tf_op jit(solution)/shard_map/ppermute | solution.py:31
  158.2 0.9 collective-permute-done.15
  160.2 17.0 %all-gather = bf16[384,1024]{1,0:T(8,128)(2,1)} all-gather(bf16[96,1024]{1,0:T(8,128)(2,1)S(1)} %copy.84), channel_id=2, replica_groups=mesh['state_0'=4,'state_1'=4,'space'=32] {'state_0'}, dimensions={0}, use_global_device_ids=true | all-gather | bytes 983040 | tf_op jit(solution)/shard_map/all_gather | solution.py:43
  177.3 6.4 %collective-permute-start.16 = (bf16[96,128]{0,1:T(8,128)(2,1)S(1)}, bf16[96,128]{0,1:T(8,128)(2,1)S(1)}, u32[]{:S(2)}, u32[]{:S(2)}) collective-permute-start(bf16[96,128]{0,1:T(8,128)(2,1)S(1)} %get-tuple-element.145), channel_id=1, source_target_pairs={{0,1},{1,2},{2,3},{3,4},{4,5},{5,6},{6,7},{7,8},{8,9},{9,10},{10,1... | collective-permute-start | bytes 73736 | tf_op jit(solution)/shard_map/ppermute | solution.py:22
  183.6 1.3 collective-permute-start.17
  184.9 9.2 %collective-permute-done.17 = bf16[96,128]{0,1:T(8,128)(2,1)S(1)} collective-permute-done((bf16[96,128]{0,1:T(8,128)(2,1)S(1)}, bf16[96,128]{0,1:T(8,128)(2,1)S(1)}, u32[]{:S(2)}, u32[]{:S(2)}) %collective-permute-start.17) | collective-permute-done | bytes 24608 | tf_op jit(solution)/shard_map/ppermute | solution.py:23
  194.2 3.2 %gather_fusion.4 = bf16[1024,96]{1,0:T(8,128)(2,1)S(1)} fusion(bf16[96,1280]{0,1:T(8,128)(2,1)S(1)} %pad_maximum_fusion.5, s32[1024]{0:T(1024)S(1)} %broadcast_clamp_fusion), kind=kCustom, calls=%fused_computation.4 | custom fusion | bytes 397312 | tf_op jit(solution)/shard_map/gather | solution.py:78
  198.1 6.2 %scatter_custom_fusion.4 = f32[96,1280]{0,1:T(8,128)S(1)} fusion(s32[1024]{0:T(1024)S(1)} %bitcast.96, f32[1024,96]{1,0:T(8,128)S(1)} %copy.82, f32[]{:T(128)} %constant.238.clone.1), kind=kCustom, calls=%fused_computation.56 | custom fusion | flops 98304 | bytes 491524 | tf_op jit(solution)/shard_map/scatter-add | solution.py:81
  204.3 1.3 collective-permute-start.18
  205.7 9.1 %collective-permute-start.19 = (f32[96,128]{0,1:T(8,128)S(1)}, f32[96,128]{0,1:T(8,128)S(1)}, u32[]{:S(2)}, u32[]{:S(2)}) collective-permute-start(f32[96,128]{0,1:T(8,128)S(1)} %get-tuple-element.135), channel_id=1, source_target_pairs={{0,1},{1,2},{2,3},{3,4},{4,5},{5,6},{6,7},{7,8},{8,9},{9,10},{10,1... | collective-permute-start | bytes 147464 | tf_op jit(solution)/shard_map/ppermute | solution.py:31
  214.8 0.9 collective-permute-done.19
  216.3 40.3 %all-gather.3.cloned.1.call-done = bf16[16,96,1024]{2,1,0:T(8,128)(2,1)} async-done(((bf16[4,96,1024]{2,1,0:T(8,128)(2,1)}), bf16[16,96,1024]{2,1,0:T(8,128)(2,1)}) %all-gather.3.cloned.1.call-update) | async-done | bytes 3145744 | tf_op jit(solution)/shard_map/all_gather | solution.py:43
  256.6 2.3 copy.79
  258.9 1.1 fusion
  260.0 1.4 fusion.1
  261.7 39.9 %all_to_all.5 = bf16[32,192,48]{1,2,0:T(8,128)(2,1)S(1)} all-to-all(bf16[32,192,48]{1,2,0:T(8,128)(2,1)S(1)} %bitcast.79), channel_id=1, replica_groups=mesh['state_0'=4,'state_1'=4,'space'=32] {'space'}, dimensions={0} | all-to-all | bytes 1179648 | tf_op jit(solution)/shard_map/all_to_all | solution.py:62
  (82 shorter events, 10.3 us)
Async XLA Ops:
  7.2 14.3 %copy-start = (bf16[2,512,512]{2,1,0:T(8,128)(2,1)S(1)}, bf16[2,512,512]{2,1,0:T(8,128)(2,1)}, u32[]{:S(2)}) copy-start(bf16[2,512,512]{2,1,0:T(8,128)(2,1)} %param.25) | copy-start | bytes 3145732
  7.2 249.4 %all-gather.3.cloned.1.call-start = ((), (), s32[]{:S(2)}) async-start(), calls=%async_computation.1 | async-start | bytes 3932160 | tf_op jit(solution)/shard_map/all_gather | solution.py:43
  8.4 3.8 %collective-permute-start = (bf16[96,128]{0,1:T(8,128)(2,1)S(1)}, bf16[96,128]{0,1:T(8,128)(2,1)S(1)}, u32[]{:S(2)}, u32[]{:S(2)}) collective-permute-start(bf16[96,128]{0,1:T(8,128)(2,1)S(1)} %get-tuple-element.153), channel_id=1, source_target_pairs={{0,1},{1,2},{2,3},{3,4},{4,5},{5,6},{6,7},{7,8},{8,9},{9,10},{10,1... | collective-permute-start | bytes 73736 | tf_op jit(solution)/shard_map/ppermute | solution.py:22
  10.2 7.8 %collective-permute-start.1 = (bf16[96,128]{0,1:T(8,128)(2,1)S(1)}, bf16[96,128]{0,1:T(8,128)(2,1)S(1)}, u32[]{:S(2)}, u32[]{:S(2)}) collective-permute-start(bf16[96,128]{0,1:T(8,128)(2,1)S(1)} %get-tuple-element.154), channel_id=1, source_target_pairs={{1,0},{2,1},{3,2},{4,3},{5,4},{6,5},{7,6},{8,7},{9,8},{10,9},{11,1... | collective-permute-start | bytes 73736 | tf_op jit(solution)/shard_map/ppermute | solution.py:23
  21.3 19.9 %copy-start.2 = (f32[1024]{0:T(1024)S(1)}, f32[1024]{0:T(1024)}, u32[]{:S(2)}) copy-start(f32[1024]{0:T(1024)} %param.27) | copy-start | bytes 12292
  28.2 11.4 %collective-permute-start.2 = (f32[96,128]{0,1:T(8,128)S(1)}, f32[96,128]{0,1:T(8,128)S(1)}, u32[]{:S(2)}, u32[]{:S(2)}) collective-permute-start(f32[96,128]{0,1:T(8,128)S(1)} %get-tuple-element.144), channel_id=1, source_target_pairs={{1,0},{2,1},{3,2},{4,3},{5,4},{6,5},{7,6},{8,7},{9,8},{10,9},{11,1... | collective-permute-start | bytes 147464 | tf_op jit(solution)/shard_map/ppermute | solution.py:31
  30.2 10.3 %collective-permute-start.3 = (f32[96,128]{0,1:T(8,128)S(1)}, f32[96,128]{0,1:T(8,128)S(1)}, u32[]{:S(2)}, u32[]{:S(2)}) collective-permute-start(f32[96,128]{0,1:T(8,128)S(1)} %get-tuple-element.143), channel_id=1, source_target_pairs={{0,1},{1,2},{2,3},{3,4},{4,5},{5,6},{6,7},{7,8},{8,9},{9,10},{10,1... | collective-permute-start | bytes 147464 | tf_op jit(solution)/shard_map/ppermute | solution.py:31
  41.4 9.8 %collective-permute-start.4 = (bf16[96,128]{0,1:T(8,128)(2,1)S(1)}, bf16[96,128]{0,1:T(8,128)(2,1)S(1)}, u32[]{:S(2)}, u32[]{:S(2)}) collective-permute-start(bf16[96,128]{0,1:T(8,128)(2,1)S(1)} %get-tuple-element.151), channel_id=1, source_target_pairs={{0,1},{1,2},{2,3},{3,4},{4,5},{5,6},{6,7},{7,8},{8,9},{9,10},{10,1... | collective-permute-start | bytes 73736 | tf_op jit(solution)/shard_map/ppermute | solution.py:22
  49.9 9.0 %collective-permute-start.5 = (bf16[96,128]{0,1:T(8,128)(2,1)S(1)}, bf16[96,128]{0,1:T(8,128)(2,1)S(1)}, u32[]{:S(2)}, u32[]{:S(2)}) collective-permute-start(bf16[96,128]{0,1:T(8,128)(2,1)S(1)} %get-tuple-element.152), channel_id=1, source_target_pairs={{1,0},{2,1},{3,2},{4,3},{5,4},{6,5},{7,6},{8,7},{9,8},{10,9},{11,1... | collective-permute-start | bytes 73736 | tf_op jit(solution)/shard_map/ppermute | solution.py:23
  69.2 10.4 %collective-permute-start.6 = (f32[96,128]{0,1:T(8,128)S(1)}, f32[96,128]{0,1:T(8,128)S(1)}, u32[]{:S(2)}, u32[]{:S(2)}) collective-permute-start(f32[96,128]{0,1:T(8,128)S(1)} %get-tuple-element.142), channel_id=1, source_target_pairs={{1,0},{2,1},{3,2},{4,3},{5,4},{6,5},{7,6},{8,7},{9,8},{10,9},{11,1... | collective-permute-start | bytes 147464 | tf_op jit(solution)/shard_map/ppermute | solution.py:31
  70.5 10.0 %collective-permute-start.7 = (f32[96,128]{0,1:T(8,128)S(1)}, f32[96,128]{0,1:T(8,128)S(1)}, u32[]{:S(2)}, u32[]{:S(2)}) collective-permute-start(f32[96,128]{0,1:T(8,128)S(1)} %get-tuple-element.141), channel_id=1, source_target_pairs={{0,1},{1,2},{2,3},{3,4},{4,5},{5,6},{6,7},{7,8},{8,9},{9,10},{10,1... | collective-permute-start | bytes 147464 | tf_op jit(solution)/shard_map/ppermute | solution.py:31
  81.4 9.3 %collective-permute-start.8 = (bf16[96,128]{0,1:T(8,128)(2,1)S(1)}, bf16[96,128]{0,1:T(8,128)(2,1)S(1)}, u32[]{:S(2)}, u32[]{:S(2)}) collective-permute-start(bf16[96,128]{0,1:T(8,128)(2,1)S(1)} %get-tuple-element.149), channel_id=1, source_target_pairs={{0,1},{1,2},{2,3},{3,4},{4,5},{5,6},{6,7},{7,8},{8,9},{9,10},{10,1... | collective-permute-start | bytes 73736 | tf_op jit(solution)/shard_map/ppermute | solution.py:22
  89.4 8.9 %collective-permute-start.9 = (bf16[96,128]{0,1:T(8,128)(2,1)S(1)}, bf16[96,128]{0,1:T(8,128)(2,1)S(1)}, u32[]{:S(2)}, u32[]{:S(2)}) collective-permute-start(bf16[96,128]{0,1:T(8,128)(2,1)S(1)} %get-tuple-element.150), channel_id=1, source_target_pairs={{1,0},{2,1},{3,2},{4,3},{5,4},{6,5},{7,6},{8,7},{9,8},{10,9},{11,1... | collective-permute-start | bytes 73736 | tf_op jit(solution)/shard_map/ppermute | solution.py:23
  108.5 10.4 %collective-permute-start.10 = (f32[96,128]{0,1:T(8,128)S(1)}, f32[96,128]{0,1:T(8,128)S(1)}, u32[]{:S(2)}, u32[]{:S(2)}) collective-permute-start(f32[96,128]{0,1:T(8,128)S(1)} %get-tuple-element.140), channel_id=1, source_target_pairs={{1,0},{2,1},{3,2},{4,3},{5,4},{6,5},{7,6},{8,7},{9,8},{10,9},{11,1... | collective-permute-start | bytes 147464 | tf_op jit(solution)/shard_map/ppermute | solution.py:31
  109.8 10.0 %collective-permute-start.11 = (f32[96,128]{0,1:T(8,128)S(1)}, f32[96,128]{0,1:T(8,128)S(1)}, u32[]{:S(2)}, u32[]{:S(2)}) collective-permute-start(f32[96,128]{0,1:T(8,128)S(1)} %get-tuple-element.139), channel_id=1, source_target_pairs={{0,1},{1,2},{2,3},{3,4},{4,5},{5,6},{6,7},{7,8},{8,9},{9,10},{10,1... | collective-permute-start | bytes 147464 | tf_op jit(solution)/shard_map/ppermute | solution.py:31
  120.7 9.5 %collective-permute-start.12 = (bf16[96,128]{0,1:T(8,128)(2,1)S(1)}, bf16[96,128]{0,1:T(8,128)(2,1)S(1)}, u32[]{:S(2)}, u32[]{:S(2)}) collective-permute-start(bf16[96,128]{0,1:T(8,128)(2,1)S(1)} %get-tuple-element.147), channel_id=1, source_target_pairs={{0,1},{1,2},{2,3},{3,4},{4,5},{5,6},{6,7},{7,8},{8,9},{9,10},{10,1... | collective-permute-start | bytes 73736 | tf_op jit(solution)/shard_map/ppermute | solution.py:22
  128.7 8.9 %collective-permute-start.13 = (bf16[96,128]{0,1:T(8,128)(2,1)S(1)}, bf16[96,128]{0,1:T(8,128)(2,1)S(1)}, u32[]{:S(2)}, u32[]{:S(2)}) collective-permute-start(bf16[96,128]{0,1:T(8,128)(2,1)S(1)} %get-tuple-element.148), channel_id=1, source_target_pairs={{1,0},{2,1},{3,2},{4,3},{5,4},{6,5},{7,6},{8,7},{9,8},{10,9},{11,1... | collective-permute-start | bytes 73736 | tf_op jit(solution)/shard_map/ppermute | solution.py:23
  147.8 10.4 %collective-permute-start.14 = (f32[96,128]{0,1:T(8,128)S(1)}, f32[96,128]{0,1:T(8,128)S(1)}, u32[]{:S(2)}, u32[]{:S(2)}) collective-permute-start(f32[96,128]{0,1:T(8,128)S(1)} %get-tuple-element.138), channel_id=1, source_target_pairs={{1,0},{2,1},{3,2},{4,3},{5,4},{6,5},{7,6},{8,7},{9,8},{10,9},{11,1... | collective-permute-start | bytes 147464 | tf_op jit(solution)/shard_map/ppermute | solution.py:31
  149.1 10.0 %collective-permute-start.15 = (f32[96,128]{0,1:T(8,128)S(1)}, f32[96,128]{0,1:T(8,128)S(1)}, u32[]{:S(2)}, u32[]{:S(2)}) collective-permute-start(f32[96,128]{0,1:T(8,128)S(1)} %get-tuple-element.137), channel_id=1, source_target_pairs={{0,1},{1,2},{2,3},{3,4},{4,5},{5,6},{6,7},{7,8},{8,9},{9,10},{10,1... | collective-permute-start | bytes 147464 | tf_op jit(solution)/shard_map/ppermute | solution.py:31
  160.2 37.7 %copy-start.1 = (bf16[96,1024]{1,0:T(8,128)(2,1)}, bf16[96,1024]{1,0:T(8,128)(2,1)S(1)}, u32[]{:S(2)}) copy-start(bf16[96,1024]{1,0:T(8,128)(2,1)S(1)} %copy.84) | copy-start | bytes 589828
  177.3 7.7 %collective-permute-start.16 = (bf16[96,128]{0,1:T(8,128)(2,1)S(1)}, bf16[96,128]{0,1:T(8,128)(2,1)S(1)}, u32[]{:S(2)}, u32[]{:S(2)}) collective-permute-start(bf16[96,128]{0,1:T(8,128)(2,1)S(1)} %get-tuple-element.145), channel_id=1, source_target_pairs={{0,1},{1,2},{2,3},{3,4},{4,5},{5,6},{6,7},{7,8},{8,9},{9,10},{10,1... | collective-permute-start | bytes 73736 | tf_op jit(solution)/shard_map/ppermute | solution.py:22
  183.6 10.5 %collective-permute-start.17 = (bf16[96,128]{0,1:T(8,128)(2,1)S(1)}, bf16[96,128]{0,1:T(8,128)(2,1)S(1)}, u32[]{:S(2)}, u32[]{:S(2)}) collective-permute-start(bf16[96,128]{0,1:T(8,128)(2,1)S(1)} %get-tuple-element.146), channel_id=1, source_target_pairs={{1,0},{2,1},{3,2},{4,3},{5,4},{6,5},{7,6},{8,7},{9,8},{10,9},{11,1... | collective-permute-start | bytes 73736 | tf_op jit(solution)/shard_map/ppermute | solution.py:23
  204.3 10.4 %collective-permute-start.18 = (f32[96,128]{0,1:T(8,128)S(1)}, f32[96,128]{0,1:T(8,128)S(1)}, u32[]{:S(2)}, u32[]{:S(2)}) collective-permute-start(f32[96,128]{0,1:T(8,128)S(1)} %get-tuple-element.136), channel_id=1, source_target_pairs={{1,0},{2,1},{3,2},{4,3},{5,4},{6,5},{7,6},{8,7},{9,8},{10,9},{11,1... | collective-permute-start | bytes 147464 | tf_op jit(solution)/shard_map/ppermute | solution.py:31
  205.7 10.0 %collective-permute-start.19 = (f32[96,128]{0,1:T(8,128)S(1)}, f32[96,128]{0,1:T(8,128)S(1)}, u32[]{:S(2)}, u32[]{:S(2)}) collective-permute-start(f32[96,128]{0,1:T(8,128)S(1)} %get-tuple-element.135), channel_id=1, source_target_pairs={{0,1},{1,2},{2,3},{3,4},{4,5},{5,6},{6,7},{7,8},{8,9},{9,10},{10,1... | collective-permute-start | bytes 147464 | tf_op jit(solution)/shard_map/ppermute | solution.py:31
Sparse Core Ops, SparseCore 0:
  177.4 79.1 all-gather.2
where the time goes:
time: 310 us; the launch traced here: 309 us
  starting transfers between devices  91.4 us (29%)
  waiting for transfers between devices  82.3 us (27%)
  blocking collectives  57 us (18%)
  other arithmetic  37.1 us (12%)
  local copies, waits for them, and re-layouts  22.7 us (7%)
  between operations  14.8 us (5%)
  matrix products  3.97 us (1%)
    ppermute x10, starting transfers between devices, shifted(): return lax.ppermute(block, axis, route)  52.2 us
    all_gather x1, waiting for transfers between devices, gather_in_order(): pieces = lax.all_gather(pieces, axes[k], axis=0, tiled=True)  40.3 us
    all_to_all x1, blocking collectives, summed_on_arrival(): lax.all_to_all(split_up(shard, dim, length), axis, 0, 0, tiled=True)  39.9 us
    ppermute x5, waiting for transfers between devices, padded(): after = lax.ppermute(leading, axis, down)  37.7 us
    ppermute x5, starting transfers between devices, padded(): before = lax.ppermute(last, axis, up)  32.6 us
    scatter-add x5, other arithmetic, apply_hamiltonian(): summed.at[:, local_index.reshape(-1)]  30.9 us
    all_gather x1, blocking collectives, gather_in_order(): pieces = lax.all_gather(pieces, axes[k], axis=0, tiled=True)  17 us
    gather x10, local copies, waits for them, and re-layouts, apply_hamiltonian(): picked = extended[:, local_index]  16.7 us
  transfers between devices with their start and end apart: 21, of which 11 were waited for; matrix products, arithmetic and copies ran while one was open for 4% of the time, Pallas kernels for 0%

commit v1 on v0

v1 whole, which is shorter than its diff:
```python
import functools

import jax
import jax.numpy as jnp
from jax import lax
from jax.experimental import pallas as pl
from jax.experimental.pallas import tpu as pltpu
from jax.sharding import Mesh
from jax.sharding import PartitionSpec as P

DEGREE = 4
STATE = ("state_0", "state_1")
CENTER = 3.0
HALF = 3.5
F32 = jnp.float32
BF16 = jnp.bfloat16
MESH_ID = pl.DeviceIdType.MESH


def joined_along(pieces, dim):
    shape = list(pieces.shape[1:])
    shape[dim] *= pieces.shape[0]
    return jnp.moveaxis(pieces, 0, dim).reshape(shape)


def gather_in_order(shard, axes, turns):
    pieces = shard[None]
    for k in turns:
        pieces = lax.all_gather(pieces, axes[k], axis=0, tiled=True)
    carried = [lax.axis_size(axes[k]) for k in reversed(turns)]
    pieces = pieces.reshape(*carried, *shard.shape)
    turned = sorted(range(len(turns)), key=lambda place: turns[len(turns) - 1 - place])
    return pieces.transpose(*turned, *range(len(turns), pieces.ndim)).reshape(-1, *shard.shape)


def gathered_by_axis(shard, axes, turns, dim):
    return joined_along(gather_in_order(shard, axes, turns), dim)


def split_up(shard, dim, length):
    shape = shard.shape
    pieces = shard.reshape(*shape[:dim], length, shape[dim] // length, *shape[dim + 1 :])
    return jnp.moveaxis(pieces, dim, 0)


def summed_on_arrival(shard, axis, dim):
    length = lax.axis_size(axis)
    pieces = lax.all_to_all(split_up(shard, dim, length), axis, 0, 0, tiled=True)
    return jnp.sum(pieces.astype(jnp.float32), axis=0)


def in_one_piece(arrays, axis, dim, along):
    both = jnp.concatenate(arrays, axis=along)
    filled, at, done = (summed_on_arrival(both, axis, dim), 0, [])
    for a in arrays:
        done.append(lax.slice_in_dim(filled, at, at + a.shape[along], axis=along))
        at += a.shape[along]
    return tuple(done)


def filter_kernel(
    states_ref, cells_ref, conn_ref, pot_ref,
    filt_ref, energy_ref,
    pick_ref, put_ref, v_ref, acc_ref, part_ref, snd_ref, rcv_ref, esnd_ref, ercv_ref, ssem, rsem,
):
    rows, nodes = states_ref.shape
    cells, local = conn_ref.shape
    ext = pick_ref.shape[0]
    rim = (ext - nodes) // 2
    zone = 2 * rim
    inner = slice(zone, ext - zone)
    zones = (slice(0, zone), slice(ext - zone, ext))
    ring = lax.axis_size("space")
    me = lax.axis_index("space")
    left, right = lax.rem(me + ring - 1, ring), lax.rem(me + 1, ring)
    to = (left, right)

    barrier = pltpu.get_barrier_semaphore()
    for near in to:
        pl.semaphore_signal(barrier, inc=1, device_id={"space": near}, device_id_type=MESH_ID)

    offset = me * nodes - rim
    v_ref[0, :, rim : rim + nodes] = states_ref[...]

    tile = 128
    for c in range(cells):
        named = conn_ref[c : c + 1, :] - offset

        @pl.loop(0, ext // tile)
        def _(r):
            start = pl.multiple_of(r * tile, tile)
            node = lax.broadcasted_iota(jnp.int32, (tile, local), 0) + start
            pick_ref[pl.ds(start, tile), c * local : (c + 1) * local] = jnp.where(
                node == named, 1.0, 0.0
            ).astype(BF16)

    pl.semaphore_wait(barrier, 2)

    def copy(step, side, src, dst):
        return pltpu.make_async_remote_copy(
            src_ref=src, dst_ref=dst, send_sem=ssem.at[step, side], recv_sem=rsem.at[step, 1 - side],
            device_id={"space": to[side]}, device_id_type=MESH_ID,
        )

    flights = [[] for _ in range(DEGREE + 2)]
    flights[0] = [
        copy(0, 0, states_ref.at[:, pl.ds(0, rim)], v_ref.at[0, :, pl.ds(ext - rim, rim)]),
        copy(0, 1, states_ref.at[:, pl.ds(nodes - rim, rim)], v_ref.at[0, :, pl.ds(0, rim)]),
    ]
    for f in flights[0]:
        f.start()

    for c in range(cells):
        named = jnp.transpose(jnp.broadcast_to(conn_ref[c : c + 1, :] - offset, (tile, local)))

        @pl.loop(0, ext // tile)
        def _(n):
            start = pl.multiple_of(n * tile, tile)
            node = lax.broadcasted_iota(jnp.int32, (local, tile), 1) + start
            put_ref[c * local : (c + 1) * local, pl.ds(start, tile)] = jnp.where(
                node == named, 1.0, 0.0
            ).astype(BF16)

    still = jnp.zeros((1, rim), F32)
    pot = jnp.concatenate([still, pot_ref[...], still], axis=1)

    def level(k, image, where):
        held = v_ref[k - 1, :, where].astype(F32)
        if k == 1:
            made = (image - CENTER * held) * (1.0 / HALF)
        else:
            made = (image - CENTER * held) * (2.0 / HALF) - v_ref[k - 2, :, where].astype(F32)
        v_ref[k, :, where] = made.astype(BF16)

    def product(picked):
        return jnp.concatenate(
            [
                jnp.dot(picked[:, c * local : (c + 1) * local], cells_ref[c], preferred_element_type=F32)
                for c in range(cells)
            ],
            axis=1,
        )

    def picked(k, where):
        return jnp.dot(v_ref[k, :, where], pick_ref[where, :], preferred_element_type=F32)

    for k in range(DEGREE + 1):
        acc_ref[...] = product(picked(k, inner).astype(BF16))
        for f in flights[k]:
            f.wait_recv()
        if k:
            for side in (0, 1):
                level(k, part_ref[side] + rcv_ref[k - 1, side].astype(F32), zones[side])
        late = (picked(k, zones[0]) + picked(k, zones[1])).astype(BF16)
        products = (acc_ref[...] + product(late)).astype(BF16)

        def image(where):
            placed = jnp.dot(products, put_ref[:, where], preferred_element_type=F32)
            return placed + pot[:, where] * v_ref[k, :, where].astype(F32)

        for side in (0, 1):
            mine = image(zones[side])
            part_ref[side] = mine
            if k < DEGREE:
                snd_ref[k, side] = mine.astype(BF16)
                flights[k + 1].append(copy(k + 1, side, snd_ref.at[k, side], rcv_ref.at[k, 1 - side]))
            else:
                esnd_ref[side] = mine[:, side * rim : (side + 1) * rim].astype(BF16)
                flights[k + 1].append(copy(k + 1, side, esnd_ref.at[side], ercv_ref.at[1 - side]))
            flights[k + 1][-1].start()
        if k < DEGREE:
            level(k + 1, image(inner), inner)
        else:
            filt_ref[...] = v_ref[k, :, rim : rim + nodes]
            energy_ref[:, rim : nodes - rim] = image(inner).astype(BF16)

    for f in flights[DEGREE + 1]:
        f.wait_recv()
    for side in (0, 1):
        at = slice(0, rim) if side == 0 else slice(nodes - rim, nodes)
        own = slice(rim, zone) if side == 0 else slice(0, rim)
        energy_ref[:, at] = (part_ref[side, :, own] + ercv_ref[side].astype(F32)).astype(BF16)
    for step in flights:
        for f in step:
            f.wait_send()


def filtered_states(states, cell_matrices, connectivity, potential):
    rows, nodes = states.shape
    cells, local, _ = cell_matrices.shape
    rim = local // 4
    ext = nodes + 2 * rim
    vmem = pl.BlockSpec(memory_space=pltpu.VMEM)
    return pl.pallas_call(
        filter_kernel,
        out_shape=(
            jax.ShapeDtypeStruct((rows, nodes), BF16),
            jax.ShapeDtypeStruct((rows, nodes), BF16),
        ),
        in_specs=[vmem] * 4,
        out_specs=(vmem, vmem),
        scratch_shapes=[
            pltpu.VMEM((ext, cells * local), BF16),
            pltpu.VMEM((cells * local, ext), BF16),
            pltpu.VMEM((DEGREE + 1, rows, ext), BF16),
            pltpu.VMEM((rows, cells * local), F32),
            pltpu.VMEM((2, rows, 2 * rim), F32),
            pltpu.VMEM((DEGREE, 2, rows, 2 * rim), BF16),
            pltpu.VMEM((DEGREE, 2, rows, 2 * rim), BF16),
            pltpu.VMEM((2, rows, rim), BF16),
            pltpu.VMEM((2, rows, rim), BF16),
            pltpu.SemaphoreType.DMA((DEGREE + 2, 2)),
            pltpu.SemaphoreType.DMA((DEGREE + 2, 2)),
        ],
        compiler_params=pltpu.CompilerParams(collective_id=0, has_side_effects=True),
    )(states, cell_matrices, connectivity, potential.reshape(1, -1))


def per_device(states_in, cell_matrices, connectivity, potential):
    current, energy = filtered_states(states_in, cell_matrices, connectivity, potential)
    total_nodes = states_in.shape[1] * lax.axis_size("space")
    contract = (((1,), (1,)), ((), ()))
    gathered = gathered_by_axis(current, STATE, (0, 1), 0)
    intersection = lax.dot_general(current, gathered, contract, preferred_element_type=jnp.float32)
    projected = lax.dot_general(energy, gathered, contract, preferred_element_type=jnp.float32)
    intersection = intersection / total_nodes
    projected = projected / total_nodes
    intersection, projected = in_one_piece(
        (intersection.astype(jnp.bfloat16), projected.astype(jnp.bfloat16)), "space", 1, 0
    )
    return (current, intersection, projected)


def solution(mesh):
    states = mesh.shape["state"]
    wide = 4 if states % 4 == 0 else 1
    finer = Mesh(
        mesh.devices.reshape(states // wide, wide, mesh.shape["space"]), ("state_0", "state_1", "space")
    )
    placed = (P(STATE, "space"), P("space", None, None), P("space", None), P("space"))
    return jax.shard_map(
        per_device,
        mesh=finer,
        in_specs=placed,
        out_specs=(P(STATE, "space"), P(STATE, "space"), P(STATE, "space")),
        check_vma=False,
    )
```

time: 310 us -> 170 us (0.55)
  starting transfers between devices: 91.4 us -> 0.04 us
  Pallas kernels: 0 us -> 54.7 us
  waiting for transfers between devices: 82.3 us -> 39.1 us
  other arithmetic: 37.1 us -> 0.18 us
  local copies, waits for them, and re-layouts: 22.7 us -> 3.98 us
    ppermute x20 -> x0, starting transfers between devices: 91.4 us -> none  [the longest x10 52.2 us: shifted(): return lax.ppermute(block, axis, route)]
    pallas_call x0 -> x1, Pallas kernels: none -> 54.7 us  [filtered_states(): pl.pallas_call(filter_kernel, out_shape=(jax.ShapeDtypeStruct((rows, node...]
    ppermute x20 -> x0, waiting for transfers between devices: 41.9 us -> none  [the longest x5 37.7 us: padded(): after = lax.ppermute(leading, axis, down)]
    scatter-add x15 -> x0, other arithmetic: 34.3 us -> none  [the longest x5 30.9 us: apply_hamiltonian(): summed.at[:, local_index.reshape(-1)]]
    gather x10 -> x0, local copies, waits for them, and re-layouts: 16.7 us -> none  [apply_hamiltonian(): picked = extended[:, local_index]]
  transfers between devices with their start and end apart: 21 -> 1, of which waited for: 11 -> 1; matrix products, arithmetic and copies ran while one was open for 4% -> 0% of each run, Pallas kernels for 0% -> 0%
where the time goes in v1:
time: 170 us
  blocking collectives  55.8 us (33%)
  Pallas kernels  54.7 us (32%)
  waiting for transfers between devices  39.1 us (23%)
  between operations  14.1 us (8%)
  local copies, waits for them, and re-layouts  3.98 us (2%)
  matrix products  2.19 us (1%)
    pallas_call x1, Pallas kernels, filtered_states(): pl.pallas_call(filter_kernel, out_shape=(jax.ShapeDtypeStruct((rows, node...  54.7 us
    all_to_all x1, blocking collectives, summed_on_arrival(): lax.all_to_all(split_up(shard, dim, length), axis, 0, 0, tiled=True)  40.2 us
    all_gather x1, waiting for transfers between devices, gather_in_order(): pieces = lax.all_gather(pieces, axes[k], axis=0, tiled=True)  39.1 us
    all_gather x1, blocking collectives, gather_in_order(): pieces = lax.all_gather(pieces, axes[k], axis=0, tiled=True)  15.6 us
  transfers between devices with their start and end apart: 1, of which 1 were waited for; matrix products, arithmetic and copies ran while one was open for 0% of the time, Pallas kernels for 0%

profile of v1, /device:TPU:8, one launch (start us, length us, event | category | flops | bytes accessed | tf_op | source)
XLA Modules:
  0.0 170.1 jit_solution(15253591313886957219)
XLA Ops:
  7.2 0.0 all-gather.3.cloned.1.call-start
  7.2 54.7 %shard_map.67 = (bf16[96,1024]{1,0:T(8,128)(2,1)}, bf16[96,1024]{1,0:T(8,128)(2,1)}) custom-call(bf16[96,1024]{1,0:T(8,128)(2,1)} %states_ref.1, bf16[2,512,512]{2,1,0:T(8,128)(2,1)} %cells_ref.1, s32[2,512]{1,0:T(2,128)} %conn_ref.1, f32[1,1024]{1,0:T(1,128)} %bitcast.18), custom_call_target="tpu_custom_call" | custom-call | tf_op jit(solution)/shard_map/pallas_call | solution.py:194
  62.0 15.6 %all-gather = bf16[384,1024]{1,0:T(8,128)(2,1)} all-gather(bf16[96,1024]{1,0:T(8,128)(2,1)} %get-tuple-element.12), channel_id=2, replica_groups=mesh['state_0'=4,'state_1'=4,'space'=32] {'state_0'}, dimensions={0}, use_global_device_ids=true | all-gather | bytes 983040 | tf_op jit(solution)/shard_map/all_gather | solution.py:29
  77.5 0.0 all-gather.3.cloned.1.call-update
  77.6 39.1 %all-gather.3.cloned.1.call-done = bf16[16,96,1024]{2,1,0:T(8,128)(2,1)} async-done(((bf16[4,96,1024]{2,1,0:T(8,128)(2,1)}), bf16[16,96,1024]{2,1,0:T(8,128)(2,1)}) %all-gather.3.cloned.1.call-update) | async-done | bytes 3145744 | tf_op jit(solution)/shard_map/all_gather | solution.py:29
  116.6 0.0 copy-start
  116.6 2.3 %copy.10 = bf16[4,4,96,1024]{3,2,1,0:T(8,128)(2,1)S(1)} copy(bf16[4,4,96,1024]{3,2,0,1:T(8,128)(2,1)} %bitcast.15) | data formatting | bytes 6291456 | tf_op jit(solution)/shard_map/transpose | solution.py:33
  119.0 0.0 copy-start.1
  119.0 0.0 copy-done
  119.0 1.1 fusion
  120.1 0.0 copy-done.1
  120.1 1.1 fusion.1
  121.3 0.3 copy.11
  121.5 40.2 %all_to_all.5 = bf16[32,192,48]{1,2,0:T(8,128)(2,1)S(1)} all-to-all(bf16[32,192,48]{1,2,0:T(8,128)(2,1)S(1)} %bitcast.17), channel_id=1, replica_groups=mesh['state_0'=4,'state_1'=4,'space'=32] {'space'}, dimensions={0} | all-to-all | bytes 1179648 | tf_op jit(solution)/shard_map/all_to_all | solution.py:48
  161.7 0.1 convert_reduce_fusion
  161.8 0.7 fusion.2
  162.5 0.7 copy.13
  (1 shorter events, 0.0 us)
Async XLA Ops:
  7.2 109.5 %all-gather.3.cloned.1.call-start = ((), (), s32[]{:S(2)}) async-start(), calls=%async_computation.1 | async-start | bytes 3932160 | tf_op jit(solution)/shard_map/all_gather | solution.py:29
  116.6 2.4 %copy-start = (bf16[96,1024]{1,0:T(8,128)(2,1)S(1)}, bf16[96,1024]{1,0:T(8,128)(2,1)}, u32[]{:S(2)}) copy-start(bf16[96,1024]{1,0:T(8,128)(2,1)} %get-tuple-element.12) | copy-start | bytes 589828
  119.0 1.1 copy-start.1
Sparse Core Ops, SparseCore 0:
  77.7 38.8 all-gather.2

commit v2 on v1

v2 whole, which is shorter than its diff:
```python
import jax
import jax.numpy as jnp
from jax import lax
from jax.experimental import pallas as pl
from jax.experimental.pallas import tpu as pltpu
from jax.sharding import Mesh
from jax.sharding import PartitionSpec as P

DEGREE = 4
WIDE = 4
STATE = ("state_0", "state_1")
CENTER = 3.0
HALF = 3.5
F32 = jnp.float32
BF16 = jnp.bfloat16
MESH_ID = pl.DeviceIdType.MESH
TRANSPOSED = (((1,), (1,)), ((), ()))


def kernel(
    states_ref, cells_ref, conn_ref, pot_ref,
    filt_ref, inter_ref, proj_ref,
    pick_ref, put_ref, v_ref, acc_ref, part_ref, snd_ref, rcv_ref, esnd_ref, ercv_ref,
    row_ref, col_ref, sum_ref, csnd_ref, crcv_ref, psnd_ref, prcv_ref,
    ssem, rsem, lsend, lrecv, wsend, wrecv, csend, crecv, psend, precv,
):
    rows, nodes = states_ref.shape
    cells, local = conn_ref.shape
    ext = pick_ref.shape[0]
    rim = (ext - nodes) // 2
    zone = 2 * rim
    inner = slice(zone, ext - zone)
    zones = (slice(0, zone), slice(ext - zone, ext))
    half = rows // 2
    ring, line, wide = lax.axis_size("space"), lax.axis_size("state_0"), lax.axis_size("state_1")
    chips = ring // 2
    me, a, b = lax.axis_index("space"), lax.axis_index("state_0"), lax.axis_index("state_1")
    chip, core = me // 2, lax.rem(me, 2)
    to = (lax.rem(me + ring - 1, ring), lax.rem(me + 1, ring))
    beside = (lax.rem(b + wide - 1, wide), lax.rem(b + 1, wide))
    opposite = lax.rem(b + 2, wide)
    sibling = me + 1 - 2 * core
    source = lax.rem(chip, wide)
    keeps = b == source

    barrier = pltpu.get_barrier_semaphore()

    def greet(**device):
        pl.semaphore_signal(barrier, inc=1, device_id=device, device_id_type=MESH_ID)

    for side in (0, 1):
        greet(space=to[side])
        greet(state_1=beside[side])

    @pl.when(a > 0)
    def _():
        greet(state_0=a - 1)

    @pl.when(a < line - 1)
    def _():
        greet(state_0=a + 1)

    for p in range(chips):

        @pl.when(jnp.logical_not(keeps & (chip == p)))
        def _():
            greet(state_1=source, space=2 * p + core)

    offset = me * nodes - rim
    v_ref[0, :, rim : rim + nodes] = states_ref[...]

    tile = rim
    for c in range(cells):
        named = conn_ref[c : c + 1, :] - offset

        @pl.loop(0, ext // tile)
        def _(r):
            start = pl.multiple_of(r * tile, tile)
            node = lax.broadcasted_iota(jnp.int32, (tile, local), 0) + start
            pick_ref[pl.ds(start, tile), c * local : (c + 1) * local] = jnp.where(
                node == named, 1.0, 0.0
            ).astype(BF16)

    greeted = jnp.int32(4 + chips) + (a > 0).astype(jnp.int32) + (a < line - 1).astype(jnp.int32)
    pl.semaphore_wait(barrier, greeted - keeps.astype(jnp.int32))

    def copy(step, side, src, dst):
        return pltpu.make_async_remote_copy(
            src_ref=src, dst_ref=dst, send_sem=ssem.at[step, side], recv_sem=rsem.at[step, 1 - side],
            device_id={"space": to[side]}, device_id_type=MESH_ID,
        )

    flights = [[] for _ in range(DEGREE + 2)]
    flights[0] = [
        copy(0, 0, states_ref.at[:, pl.ds(0, rim)], v_ref.at[0, :, pl.ds(ext - rim, rim)]),
        copy(0, 1, states_ref.at[:, pl.ds(nodes - rim, rim)], v_ref.at[0, :, pl.ds(0, rim)]),
    ]
    for f in flights[0]:
        f.start()

    for c in range(cells):
        named = jnp.transpose(jnp.broadcast_to(conn_ref[c : c + 1, :] - offset, (tile, local)))

        @pl.loop(0, ext // tile)
        def _(n):
            start = pl.multiple_of(n * tile, tile)
            node = lax.broadcasted_iota(jnp.int32, (local, tile), 1) + start
            put_ref[c * local : (c + 1) * local, pl.ds(start, tile)] = jnp.where(
                node == named, 1.0, 0.0
            ).astype(BF16)

    still = jnp.zeros((1, rim), F32)
    pot = jnp.concatenate([still, pot_ref[...], still], axis=1)

    def level(k, image, where):
        held = v_ref[k - 1, :, where].astype(F32)
        if k == 1:
            made = (image - CENTER * held) * (1.0 / HALF)
        else:
            made = (image - CENTER * held) * (2.0 / HALF) - v_ref[k - 2, :, where].astype(F32)
        v_ref[k, :, where] = made.astype(BF16)

    def product(picked):
        return jnp.concatenate(
            [
                jnp.dot(picked[:, c * local : (c + 1) * local], cells_ref[c], preferred_element_type=F32)
                for c in range(cells)
            ],
            axis=1,
        )

    def picked(k, where):
        return jnp.dot(v_ref[k, :, where], pick_ref[where, :], preferred_element_type=F32)

    parts = ((rim, nodes - zone), (0, rim), (nodes - rim, rim))

    def along(way, block, part):
        block = lax.rem(block + line, line)
        spot = col_ref.at[block, :, pl.ds(*parts[part])]
        return pltpu.make_async_remote_copy(
            src_ref=spot, dst_ref=spot, send_sem=lsend.at[way, block, part], recv_sem=lrecv.at[block, part],
            device_id={"state_0": lax.rem(a + line + 2 * way - 1, line)}, device_id_type=MESH_ID,
        )

    def goes(way, hop):
        return (a - hop >= 0) & (a + 1 < line) if way else (a + hop < line) & (a >= 1)

    def come(way, hop):
        return a - hop >= 0 if way else a + hop < line

    def pass_along(hop, part):
        for way in (0, 1):
            block = a - hop if way else a + hop
            if hop:

                @pl.when(come(way, hop))
                def _():
                    along(way, block, part).wait_recv()

            @pl.when(goes(way, hop))
            def _():
                along(way, block, part).start()

    def around(turn, kind, part):
        block = (b, b, beside[0], beside[1])[turn]
        first, count = ((0, rows), (0, rows), (0, half), (half, half))[turn]
        spot = row_ref.at[block, pl.ds(kind * rows + first, count), pl.ds(*parts[part])]
        return pltpu.make_async_remote_copy(
            src_ref=spot, dst_ref=spot, send_sem=wsend.at[turn, kind, part], recv_sem=wrecv.at[turn, kind, part],
            device_id={"state_1": beside[1 - turn % 2]}, device_id_type=MESH_ID,
        )

    def arrive(turn, kind, part):
        block = (beside[0], beside[1], opposite, opposite)[turn]
        first, count = ((0, rows), (0, rows), (0, half), (half, half))[turn]
        spot = row_ref.at[block, pl.ds(kind * rows + first, count), pl.ds(*parts[part])]
        pltpu.make_async_remote_copy(
            src_ref=spot, dst_ref=spot, send_sem=wsend.at[turn, kind, part], recv_sem=wrecv.at[turn, kind, part],
            device_id={"state_1": beside[1 - turn % 2]}, device_id_type=MESH_ID,
        ).wait_recv()

    def send_around(kind, part):
        for turn in (0, 1):
            around(turn, kind, part).start()

    def pass_around(kind, part):
        for turn in (0, 1):
            arrive(turn, kind, part)
            around(turn + 2, kind, part).start()

    def share(part):
        first, count = parts[part]
        own = v_ref[DEGREE, :, rim + first : rim + first + count]
        col_ref[a, :, first : first + count] = own
        row_ref[b, 0:rows, first : first + count] = own
        pass_along(0, part)
        send_around(0, part)

    for k in range(DEGREE + 1):
        acc_ref[...] = product(picked(k, inner).astype(BF16))
        for f in flights[k]:
            f.wait_recv()
        if k:
            for side in (0, 1):
                level(k, part_ref[side] + rcv_ref[k - 1, side].astype(F32), zones[side])
        if k == DEGREE:
            share(1)
            share(2)
        late = (picked(k, zones[0]) + picked(k, zones[1])).astype(BF16)
        products = (acc_ref[...] + product(late)).astype(BF16)

        def image(where):
            placed = jnp.dot(products, put_ref[:, where], preferred_element_type=F32)
            return placed + pot[:, where] * v_ref[k, :, where].astype(F32)

        for side in (0, 1):
            mine = image(zones[side])
            part_ref[side] = mine
            if k < DEGREE:
                snd_ref[k, side] = mine.astype(BF16)
                flights[k + 1].append(copy(k + 1, side, snd_ref.at[k, side], rcv_ref.at[k, 1 - side]))
            else:
                esnd_ref[side] = mine[:, side * rim : (side + 1) * rim].astype(BF16)
                flights[k + 1].append(copy(k + 1, side, esnd_ref.at[side], ercv_ref.at[1 - side]))
            flights[k + 1][-1].start()
        if k < DEGREE:
            level(k + 1, image(inner), inner)
        else:
            filt_ref[...] = v_ref[k, :, rim : rim + nodes]
            row_ref[b, rows : 2 * rows, rim : nodes - rim] = image(inner).astype(BF16)
            send_around(1, 0)
        if k == DEGREE - 1:
            share(0)

    pass_along(1, 0)
    pass_around(0, 0)
    for f in flights[DEGREE + 1]:
        f.wait_recv()
    for side in (0, 1):
        first = side * (nodes - rim)
        own = slice(rim, zone) if side == 0 else slice(0, rim)
        row_ref[b, rows : 2 * rows, first : first + rim] = (
            part_ref[side, :, own] + ercv_ref[side].astype(F32)
        ).astype(BF16)
        send_around(1, 1 + side)
    for part in (1, 2):
        pass_along(1, part)
        pass_around(0, part)
    for hop in range(2, max(line, 3)):
        for part in range(3):
            pass_along(hop, part)
            if hop == 2:
                pass_around(1, part)
    for kind in (0, 1):
        for part in range(3):
            for turn in (2, 3):
                arrive(turn, kind, part)

    def to_sibling(i):
        return pltpu.make_async_remote_copy(
            src_ref=csnd_ref.at[i], dst_ref=crcv_ref.at[i], send_sem=csend.at[i], recv_sem=crecv.at[i],
            device_id={"space": sibling}, device_id_type=MESH_ID,
        )

    for i in range(line):
        for j in range(wide):
            sum_ref[i, j] = lax.dot_general(col_ref[i], row_ref[j], TRANSPOSED, preferred_element_type=F32)
            csnd_ref[i, j] = sum_ref[i, j, pl.ds(pl.multiple_of((1 - core) * half, half), half), :].astype(BF16)
        to_sibling(i).start()

    def to_owner(i, j):
        return pltpu.make_async_remote_copy(
            src_ref=psnd_ref.at[i, j], dst_ref=prcv_ref.at[chip], send_sem=psend.at[i, j], recv_sem=precv.at[chip],
            device_id={"state_1": j, "space": 2 * (i * wide + b) + core}, device_id_type=MESH_ID,
        )

    def stays(i, j):
        return (b == j) & (chip == i * wide + b)

    for i in range(line):
        to_sibling(i).wait_recv()
        for j in range(wide):
            mine = sum_ref[i, j, pl.ds(pl.multiple_of(core * half, half), half), :]
            psnd_ref[i, j] = (mine + crcv_ref[i, j].astype(F32)).astype(BF16)

            @pl.when(stays(i, j))
            def _():
                prcv_ref[chip] = psnd_ref[i, j]

            @pl.when(jnp.logical_not(stays(i, j)))
            def _():
                to_owner(i, j).start()

    total = jnp.zeros((half, 2 * rows), F32)
    for p in range(chips):

        @pl.when(jnp.logical_not(keeps & (chip == p)))
        def _():
            pltpu.make_async_remote_copy(
                src_ref=prcv_ref.at[p], dst_ref=prcv_ref.at[p], send_sem=precv.at[p], recv_sem=precv.at[p],
                device_id={"space": sibling}, device_id_type=MESH_ID,
            ).wait_recv()

        total += prcv_ref[p].astype(F32)
    turned = jnp.transpose(total * (1.0 / (nodes * ring)))
    inter_ref[...] = turned[0:rows]
    proj_ref[...] = turned[rows : 2 * rows]

    for step in flights:
        for f in step:
            f.wait_send()
    for way in (0, 1):
        for hop in range(line - 1):
            for part in range(3):

                @pl.when(goes(way, hop))
                def _():
                    along(way, a - hop if way else a + hop, part).wait_send()

    for turn in range(4):
        for kind in (0, 1):
            for part in range(3):
                around(turn, kind, part).wait_send()
    for i in range(line):
        to_sibling(i).wait_send()
        for j in range(wide):

            @pl.when(jnp.logical_not(stays(i, j)))
            def _():
                to_owner(i, j).wait_send()


def per_device(states, cell_matrices, connectivity, potential):
    rows, nodes = states.shape
    cells, local, _ = cell_matrices.shape
    line, wide, ring = (lax.axis_size(name) for name in (*STATE, "space"))
    chips, half = ring // 2, rows // 2
    rim = local // 4
    ext = nodes + 2 * rim
    vmem = pl.BlockSpec(memory_space=pltpu.VMEM)
    dma = pltpu.SemaphoreType.DMA
    return pl.pallas_call(
        kernel,
        out_shape=(
            jax.ShapeDtypeStruct((rows, nodes), BF16),
            jax.ShapeDtypeStruct((rows, half), F32),
            jax.ShapeDtypeStruct((rows, half), F32),
        ),
        in_specs=[vmem] * 4,
        out_specs=(vmem, vmem, vmem),
        scratch_shapes=[
            pltpu.VMEM((ext, cells * local), BF16),
            pltpu.VMEM((cells * local, ext), BF16),
            pltpu.VMEM((DEGREE + 1, rows, ext), BF16),
            pltpu.VMEM((rows, cells * local), F32),
            pltpu.VMEM((2, rows, 2 * rim), F32),
            pltpu.VMEM((DEGREE, 2, rows, 2 * rim), BF16),
            pltpu.VMEM((DEGREE, 2, rows, 2 * rim), BF16),
            pltpu.VMEM((2, rows, rim), BF16),
            pltpu.VMEM((2, rows, rim), BF16),
            pltpu.VMEM((wide, 2 * rows, nodes), BF16),
            pltpu.VMEM((line, rows, nodes), BF16),
            pltpu.VMEM((line, wide, rows, 2 * rows), F32),
            pltpu.VMEM((line, wide, half, 2 * rows), BF16),
            pltpu.VMEM((line, wide, half, 2 * rows), BF16),
            pltpu.VMEM((line, wide, half, 2 * rows), BF16),
            pltpu.VMEM((chips, half, 2 * rows), BF16),
            dma((DEGREE + 2, 2)), dma((DEGREE + 2, 2)),
            dma((2, line, 3)), dma((line, 3)),
            dma((4, 2, 3)), dma((4, 2, 3)),
            dma((line,)), dma((line,)),
            dma((line, wide)), dma((chips,)),
        ],
        compiler_params=pltpu.CompilerParams(collective_id=0, has_side_effects=True),
    )(states, cell_matrices, connectivity, potential.reshape(1, -1))


def solution(mesh):
    line = mesh.shape["state"] // WIDE
    finer = Mesh(mesh.devices.reshape(line, WIDE, mesh.shape["space"]), (*STATE, "space"))
    placed = (P(STATE, "space"), P("space", None, None), P("space", None), P("space"))
    return jax.shard_map(
        per_device,
        mesh=finer,
        in_specs=placed,
        out_specs=(P(STATE, "space"), P(STATE, "space"), P(STATE, "space")),
        check_vma=False,
    )
```

time: 170 us -> 102 us (0.60)
  the two profiles are of different devices: /device:TPU:8 before, /device:TPU:64 now
where the time goes in v2:
time: 102 us
  Pallas kernels  97.5 us (96%)
  local copies, waits for them, and re-layouts  3.8 us (4%)
    pallas_call x1, Pallas kernels, per_device(): pl.pallas_call(kernel, out_shape=(jax.ShapeDtypeStruct((rows, nodes), BF1...  97.5 us
    pallas_call x2, local copies, waits for them, and re-layouts, per_device(): pl.pallas_call(kernel, out_shape=(jax.ShapeDtypeStruct((rows, nodes), BF1...  2.18 us

profile of v2, /device:TPU:64, one launch (start us, length us, event | category | flops | bytes accessed | tf_op | source)
XLA Modules:
  0.0 102.0 jit_solution(611814524823317371)
XLA Ops:
  0.6 97.5 %shard_map.67 = (bf16[96,1024]{1,0:T(8,128)(2,1)}, f32[96,48]{1,0:T(8,128)}, f32[96,48]{1,0:T(8,128)}) custom-call(bf16[96,1024]{1,0:T(8,128)(2,1)} %states_ref.1, bf16[2,512,512]{2,1,0:T(8,128)(2,1)} %cells_ref.1, s32[2,512]{1,0:T(2,128)} %conn_ref.1, f32[1,1024]{1,0:T(1,128)} %bitcast.1), custom_call_target="tpu_custom_call" | custom-call | tf_op jit(solution)/shard_map/pallas_call | solution.py:342
  98.2 0.0 copy-start
  98.2 1.5 %copy.7 = f32[96,48]{0,1:T(8,128)} copy(f32[96,48]{1,0:T(8,128)} %get-tuple-element.4) | data formatting | bytes 36864 | tf_op jit(solution)/shard_map/pallas_call | solution.py:342
  99.7 0.0 copy-done
  99.7 0.7 copy.8
  100.4 1.6 %copy.10 = bf16[96,1024]{1,0:T(8,128)(2,1)} copy(bf16[96,1024]{1,0:T(8,128)(2,1)} %get-tuple-element.9) | data formatting | bytes 393216
Async XLA Ops:
  98.2 1.5 %copy-start = (f32[96,48]{1,0:T(8,128)S(1)}, f32[96,48]{1,0:T(8,128)}, u32[]{:S(2)}) copy-start(f32[96,48]{1,0:T(8,128)} %get-tuple-element.5) | copy-start | bytes 55300

commit v3 on v2

--- a/solution.py
+++ b/solution.py
@@ -256,16 +256,28 @@
             for turn in (2, 3):
                 arrive(turn, kind, part)
 
+    broad = prcv_ref.shape[2]
+
     def to_sibling(i):
         return pltpu.make_async_remote_copy(
             src_ref=csnd_ref.at[i], dst_ref=crcv_ref.at[i], send_sem=csend.at[i], recv_sem=crecv.at[i],
             device_id={"space": sibling}, device_id_type=MESH_ID,
         )
 
-    for i in range(line):
+    nearest = chip // wide
+    order = [lax.rem(nearest + n, line) for n in range(line)]
+    about = [lax.rem(b + n, wide) for n in range(wide)]
+
+    for i in order:
         for j in range(wide):
-            sum_ref[i, j] = lax.dot_general(col_ref[i], row_ref[j], TRANSPOSED, preferred_element_type=F32)
-            csnd_ref[i, j] = sum_ref[i, j, pl.ds(pl.multiple_of((1 - core) * half, half), half), :].astype(BF16)
+            block = lax.dot_general(col_ref[i], row_ref[j], TRANSPOSED, preferred_element_type=F32)
+            for q in (0, 1):
+                top, deep = q * half, half // 2
+                sum_ref[i, j, q, 0:half, :] = block[top : top + half, 0:broad]
+                sum_ref[i, j, q, half : half + deep, :] = jnp.concatenate(
+                    [block[top : top + deep, broad:], block[top + deep : top + half, broad:]], axis=1
+                )
+            csnd_ref[i, j] = sum_ref[i, j, 1 - core].astype(BF16)
         to_sibling(i).start()
 
     def to_owner(i, j):
@@ -277,11 +289,10 @@
     def stays(i, j):
         return (b == j) & (chip == i * wide + b)
 
-    for i in range(line):
+    for i in order:
         to_sibling(i).wait_recv()
-        for j in range(wide):
-            mine = sum_ref[i, j, pl.ds(pl.multiple_of(core * half, half), half), :]
-            psnd_ref[i, j] = (mine + crcv_ref[i, j].astype(F32)).astype(BF16)
+        for j in about:
+            psnd_ref[i, j] = (sum_ref[i, j, core] + crcv_ref[i, j].astype(F32)).astype(BF16)
 
             @pl.when(stays(i, j))
             def _():
@@ -291,7 +302,7 @@
             def _():
                 to_owner(i, j).start()
 
-    total = jnp.zeros((half, 2 * rows), F32)
+    total = jnp.zeros(prcv_ref.shape[1:], F32)
     for p in range(chips):
 
         @pl.when(jnp.logical_not(keeps & (chip == p)))
@@ -302,9 +313,11 @@
             ).wait_recv()
 
         total += prcv_ref[p].astype(F32)
-    turned = jnp.transpose(total * (1.0 / (nodes * ring)))
-    inter_ref[...] = turned[0:rows]
-    proj_ref[...] = turned[rows : 2 * rows]
+    total *= 1.0 / (nodes * ring)
+    tail = total[half:]
+    tail = jnp.concatenate([tail[:, 0 : broad // 2], tail[:, broad // 2 :]], axis=0)
+    inter_ref[...] = total[0:half, 0:rows]
+    proj_ref[...] = jnp.concatenate([total[0:half, rows:], tail], axis=1)
 
     for step in flights:
         for f in step:
@@ -335,16 +348,17 @@
     cells, local, _ = cell_matrices.shape
     line, wide, ring = (lax.axis_size(name) for name in (*STATE, "space"))
     chips, half = ring // 2, rows // 2
+    packed = (half + half // 2, 4 * rows // 3)
     rim = local // 4
     ext = nodes + 2 * rim
     vmem = pl.BlockSpec(memory_space=pltpu.VMEM)
     dma = pltpu.SemaphoreType.DMA
-    return pl.pallas_call(
+    filtered, inter, proj = pl.pallas_call(
         kernel,
         out_shape=(
             jax.ShapeDtypeStruct((rows, nodes), BF16),
-            jax.ShapeDtypeStruct((rows, half), F32),
-            jax.ShapeDtypeStruct((rows, half), F32),
+            jax.ShapeDtypeStruct((half, rows), F32),
+            jax.ShapeDtypeStruct((half, rows), F32),
         ),
         in_specs=[vmem] * 4,
         out_specs=(vmem, vmem, vmem),
@@ -360,11 +374,11 @@
             pltpu.VMEM((2, rows, rim), BF16),
             pltpu.VMEM((wide, 2 * rows, nodes), BF16),
             pltpu.VMEM((line, rows, nodes), BF16),
-            pltpu.VMEM((line, wide, rows, 2 * rows), F32),
-            pltpu.VMEM((line, wide, half, 2 * rows), BF16),
-            pltpu.VMEM((line, wide, half, 2 * rows), BF16),
-            pltpu.VMEM((line, wide, half, 2 * rows), BF16),
-            pltpu.VMEM((chips, half, 2 * rows), BF16),
+            pltpu.VMEM((line, wide, 2, *packed), F32),
+            pltpu.VMEM((line, wide, *packed), BF16),
+            pltpu.VMEM((line, wide, *packed), BF16),
+            pltpu.VMEM((line, wide, *packed), BF16),
+            pltpu.VMEM((chips, *packed), BF16),
             dma((DEGREE + 2, 2)), dma((DEGREE + 2, 2)),
             dma((2, line, 3)), dma((line, 3)),
             dma((4, 2, 3)), dma((4, 2, 3)),
@@ -373,6 +387,7 @@
         ],
         compiler_params=pltpu.CompilerParams(collective_id=0, has_side_effects=True),
     )(states, cell_matrices, connectivity, potential.reshape(1, -1))
+    return filtered, inter.T, proj.T
 
 
 def solution(mesh):

time: 102 us -> 92.6 us (0.908)
  the two profiles are of different devices: /device:TPU:64 before, /device:TPU:88 now
where the time goes in v3:
time: 92.6 us; the launch traced here: 92.4 us
  Pallas kernels  88.8 us (96%)
  local copies, waits for them, and re-layouts  2.98 us (3%)
    pallas_call x1, Pallas kernels, per_device(): pl.pallas_call(kernel, out_shape=(jax.ShapeDtypeStruct((rows, nodes), BF1...  88.8 us
    unnamed x7, local copies, waits for them, and re-layouts  2.98 us

profile of v3, /device:TPU:88, one launch (start us, length us, event | category | flops | bytes accessed | tf_op | source)
XLA Modules:
  0.0 92.4 jit_solution(16462808471237118860)
XLA Ops:
  0.6 88.8 %shard_map.67 = (bf16[96,1024]{1,0:T(8,128)(2,1)}, f32[48,96]{1,0:T(8,128)}, f32[48,96]{1,0:T(8,128)}) custom-call(bf16[96,1024]{1,0:T(8,128)(2,1)} %states_ref.1, bf16[2,512,512]{2,1,0:T(8,128)(2,1)} %cells_ref.1, s32[2,512]{1,0:T(2,128)} %conn_ref.1, f32[1,1024]{1,0:T(1,128)} %bitcast.5), custom_call_target="tpu_custom_call" | custom-call | tf_op jit(solution)/shard_map/pallas_call | solution.py:356
  89.4 0.0 copy-start.1
  89.4 1.6 %copy.10 = bf16[96,1024]{1,0:T(8,128)(2,1)} copy(bf16[96,1024]{1,0:T(8,128)(2,1)} %get-tuple-element.12) | data formatting | bytes 393216
  91.0 0.0 copy-done.1
  91.1 0.0 copy-start
  91.1 0.6 copy.11
  91.7 0.1 copy-done
  91.8 0.6 copy.12
Async XLA Ops:
  89.4 1.6 %copy-start.1 = (f32[48,96]{1,0:T(8,128)S(1)}, f32[48,96]{1,0:T(8,128)}, u32[]{:S(2)}) copy-start(f32[48,96]{1,0:T(8,128)} %get-tuple-element.7) | copy-start | bytes 55300
  91.1 0.7 copy-start

commit v4 on v3

--- a/solution.py
+++ b/solution.py
@@ -8,6 +8,7 @@
 
 DEGREE = 4
 WIDE = 4
+GROUPS = 3
 STATE = ("state_0", "state_1")
 CENTER = 3.0
 HALF = 3.5
@@ -20,9 +21,10 @@
 def kernel(
     states_ref, cells_ref, conn_ref, pot_ref,
     filt_ref, inter_ref, proj_ref,
-    pick_ref, put_ref, v_ref, acc_ref, part_ref, snd_ref, rcv_ref, esnd_ref, ercv_ref,
+    pick_ref, put_ref, v_ref, acc_ref, potx_ref, near_ref, base_ref,
+    part_ref, snd_ref, rcv_ref, esnd_ref, ercv_ref,
     row_ref, col_ref, sum_ref, csnd_ref, crcv_ref, psnd_ref, prcv_ref,
-    ssem, rsem, lsend, lrecv, wsend, wrecv, csend, crecv, psend, precv,
+    ssem, rsem, fsend, frecv, lsend, lrecv, wsend, wrecv, csend, crecv, psend, precv,
 ):
     rows, nodes = states_ref.shape
     cells, local = conn_ref.shape
@@ -30,7 +32,6 @@
     rim = (ext - nodes) // 2
     zone = 2 * rim
     inner = slice(zone, ext - zone)
-    zones = (slice(0, zone), slice(ext - zone, ext))
     half = rows // 2
     ring, line, wide = lax.axis_size("space"), lax.axis_size("state_0"), lax.axis_size("state_1")
     chips = ring // 2
@@ -40,6 +41,7 @@
     beside = (lax.rem(b + wide - 1, wide), lax.rem(b + 1, wide))
     opposite = lax.rem(b + 2, wide)
     sibling = me + 1 - 2 * core
+    distant = lax.rem(me + ring - 1 + 2 * core, ring)
     source = lax.rem(chip, wide)
     keeps = b == source
 
@@ -84,19 +86,43 @@
     greeted = jnp.int32(4 + chips) + (a > 0).astype(jnp.int32) + (a < line - 1).astype(jnp.int32)
     pl.semaphore_wait(barrier, greeted - keeps.astype(jnp.int32))
 
-    def copy(step, side, src, dst):
-        return pltpu.make_async_remote_copy(
-            src_ref=src, dst_ref=dst, send_sem=ssem.at[step, side], recv_sem=rsem.at[step, 1 - side],
-            device_id={"space": to[side]}, device_id_type=MESH_ID,
-        )
-
-    flights = [[] for _ in range(DEGREE + 2)]
-    flights[0] = [
-        copy(0, 0, states_ref.at[:, pl.ds(0, rim)], v_ref.at[0, :, pl.ds(ext - rim, rim)]),
-        copy(0, 1, states_ref.at[:, pl.ds(nodes - rim, rim)], v_ref.at[0, :, pl.ds(0, rim)]),
-    ]
-    for f in flights[0]:
-        f.start()
+    def lanes(start, width):
+        return pl.ds(pl.multiple_of(start, rim), width)
+
+    sign = (core, 1 - core)
+    zones = tuple(lanes(n * (ext - zone), zone) for n in sign)
+    edges = tuple(n * (nodes - rim) for n in sign)
+    outer = tuple(lanes(n * rim, rim) for n in sign)
+    own = tuple(lanes((1 - n) * rim, rim) for n in sign)
+    groups = tuple(pl.ds(first, rows // GROUPS) for first in range(0, rows, rows // GROUPS))
+
+    def travel(step, side, group):
+        if step == 0:
+            src = states_ref.at[group, lanes(edges[side], rim)]
+            dst = v_ref.at[0, group, lanes((1 - sign[side]) * (ext - rim), rim)]
+        elif step <= DEGREE:
+            src, dst = snd_ref.at[step - 1, side, group], rcv_ref.at[step - 1, side, group]
+        else:
+            src, dst = esnd_ref.at[side, group], ercv_ref.at[side, group]
+        return src, dst
+
+    def afar(step, g):
+        src, dst = travel(step, 0, groups[g])
+        return pltpu.make_async_remote_copy(
+            src_ref=src, dst_ref=dst, send_sem=ssem.at[step, g], recv_sem=rsem.at[step, g],
+            device_id={"space": distant}, device_id_type=MESH_ID,
+        )
+
+    def nearby(step):
+        src, dst = travel(step, 1, pl.ds(0, rows))
+        return pltpu.make_async_remote_copy(
+            src_ref=src, dst_ref=dst, send_sem=fsend.at[step], recv_sem=frecv.at[step],
+            device_id={"space": sibling}, device_id_type=MESH_ID,
+        )
+
+    for g in range(GROUPS):
+        afar(0, g).start()
+    nearby(0).start()
 
     for c in range(cells):
         named = jnp.transpose(jnp.broadcast_to(conn_ref[c : c + 1, :] - offset, (tile, local)))
@@ -109,16 +135,19 @@
                 node == named, 1.0, 0.0
             ).astype(BF16)
 
-    still = jnp.zeros((1, rim), F32)
-    pot = jnp.concatenate([still, pot_ref[...], still], axis=1)
-
-    def level(k, image, where):
-        held = v_ref[k - 1, :, where].astype(F32)
+    potx_ref[:, 0:rim] = jnp.zeros((1, rim), F32)
+    potx_ref[:, rim : rim + nodes] = pot_ref[...]
+    potx_ref[:, ext - rim : ext] = jnp.zeros((1, rim), F32)
+
+    everyone = pl.ds(0, rows)
+
+    def level(k, image, group, where):
+        held = v_ref[k - 1, group, where].astype(F32)
         if k == 1:
             made = (image - CENTER * held) * (1.0 / HALF)
         else:
-            made = (image - CENTER * held) * (2.0 / HALF) - v_ref[k - 2, :, where].astype(F32)
-        v_ref[k, :, where] = made.astype(BF16)
+            made = (image - CENTER * held) * (2.0 / HALF) - v_ref[k - 2, group, where].astype(F32)
+        v_ref[k, group, where] = made.astype(BF16)
 
     def product(picked):
         return jnp.concatenate(
@@ -130,13 +159,26 @@
         )
 
     def picked(k, where):
-        return jnp.dot(v_ref[k, :, where], pick_ref[where, :], preferred_element_type=F32)
-
-    parts = ((rim, nodes - zone), (0, rim), (nodes - rim, rim))
+        return jnp.dot(v_ref[k, :, where], pick_ref[where, :], preferred_element_type=F32).astype(BF16)
+
+    def placed(products, where):
+        return jnp.dot(products, put_ref[:, where], preferred_element_type=F32)
+
+    def own_term(k, group, where):
+        return potx_ref[:, where] * v_ref[k, group, where].astype(F32)
+
+    through = product(pick_ref[zones[0], :])
+    near_ref[0, :, 0 : cells * local] = through.astype(BF16)
+    rest = through - near_ref[0, :, 0 : cells * local].astype(F32)
+    itself = placed(near_ref[0, :, 0 : cells * local], zones[0]) + placed(rest.astype(BF16), zones[0])
+    near_ref[1, :, 0:zone] = itself.astype(BF16)
+    near_ref[2, :, 0:zone] = (itself - near_ref[1, :, 0:zone].astype(F32)).astype(BF16)
+
+    parts = ((rim, nodes - zone), (edges[1], rim), (edges[0], rim))
 
     def along(way, block, part):
         block = lax.rem(block + line, line)
-        spot = col_ref.at[block, :, pl.ds(*parts[part])]
+        spot = col_ref.at[block, :, lanes(*parts[part])]
         return pltpu.make_async_remote_copy(
             src_ref=spot, dst_ref=spot, send_sem=lsend.at[way, block, part], recv_sem=lrecv.at[block, part],
             device_id={"state_0": lax.rem(a + line + 2 * way - 1, line)}, device_id_type=MESH_ID,
@@ -164,7 +206,7 @@
     def around(turn, kind, part):
         block = (b, b, beside[0], beside[1])[turn]
         first, count = ((0, rows), (0, rows), (0, half), (half, half))[turn]
-        spot = row_ref.at[block, pl.ds(kind * rows + first, count), pl.ds(*parts[part])]
+        spot = row_ref.at[block, pl.ds(kind * rows + first, count), lanes(*parts[part])]
         return pltpu.make_async_remote_copy(
             src_ref=spot, dst_ref=spot, send_sem=wsend.at[turn, kind, part], recv_sem=wrecv.at[turn, kind, part],
             device_id={"state_1": beside[1 - turn % 2]}, device_id_type=MESH_ID,
@@ -173,7 +215,7 @@
     def arrive(turn, kind, part):
         block = (beside[0], beside[1], opposite, opposite)[turn]
         first, count = ((0, rows), (0, rows), (0, half), (half, half))[turn]
-        spot = row_ref.at[block, pl.ds(kind * rows + first, count), pl.ds(*parts[part])]
+        spot = row_ref.at[block, pl.ds(kind * rows + first, count), lanes(*parts[part])]
         pltpu.make_async_remote_copy(
             src_ref=spot, dst_ref=spot, send_sem=wsend.at[turn, kind, part], recv_sem=wrecv.at[turn, kind, part],
             device_id={"state_1": beside[1 - turn % 2]}, device_id_type=MESH_ID,
@@ -190,59 +232,69 @@
 
     def share(part):
         first, count = parts[part]
-        own = v_ref[DEGREE, :, rim + first : rim + first + count]
-        col_ref[a, :, first : first + count] = own
-        row_ref[b, 0:rows, first : first + count] = own
+        done = v_ref[DEGREE, :, lanes(rim + first, count)]
+        col_ref[a, :, lanes(first, count)] = done
+        row_ref[b, 0:rows, lanes(first, count)] = done
         pass_along(0, part)
         send_around(0, part)
 
     for k in range(DEGREE + 1):
-        acc_ref[...] = product(picked(k, inner).astype(BF16))
-        for f in flights[k]:
-            f.wait_recv()
+        acc_ref[...] = product(picked(k, inner))
+        nearby(k).wait_recv()
         if k:
-            for side in (0, 1):
-                level(k, part_ref[side] + rcv_ref[k - 1, side].astype(F32), zones[side])
+            level(k, part_ref[1] + rcv_ref[k - 1, 1].astype(F32), everyone, zones[1])
         if k == DEGREE:
             share(1)
+        acc_ref[...] += product(picked(k, zones[1]))
+        base_ref[...] = placed(acc_ref[...].astype(BF16), zones[0])
+        for g, group in enumerate(groups):
+            afar(k, g).wait_recv()
+            if k:
+                level(k, part_ref[0, group, :] + rcv_ref[k - 1, 0, group, :].astype(F32), group, zones[0])
+            held = v_ref[k, group, zones[0]]
+            mine = base_ref[group, :] + own_term(k, group, zones[0])
+            for n in (1, 2):
+                mine += jnp.dot(held, near_ref[n, :, 0:zone], preferred_element_type=F32)
+            part_ref[0, group, :] = mine
+            if k < DEGREE:
+                snd_ref[k, 0, group, :] = mine.astype(BF16)
+            else:
+                esnd_ref[0, group, :] = part_ref[0, group, outer[0]].astype(BF16)
+            afar(k + 1, g).start()
+        if k == DEGREE:
             share(2)
-        late = (picked(k, zones[0]) + picked(k, zones[1])).astype(BF16)
-        products = (acc_ref[...] + product(late)).astype(BF16)
-
-        def image(where):
-            placed = jnp.dot(products, put_ref[:, where], preferred_element_type=F32)
-            return placed + pot[:, where] * v_ref[k, :, where].astype(F32)
-
-        for side in (0, 1):
-            mine = image(zones[side])
-            part_ref[side] = mine
-            if k < DEGREE:
-                snd_ref[k, side] = mine.astype(BF16)
-                flights[k + 1].append(copy(k + 1, side, snd_ref.at[k, side], rcv_ref.at[k, 1 - side]))
-            else:
-                esnd_ref[side] = mine[:, side * rim : (side + 1) * rim].astype(BF16)
-                flights[k + 1].append(copy(k + 1, side, esnd_ref.at[side], ercv_ref.at[1 - side]))
-            flights[k + 1][-1].start()
+        products = (acc_ref[...] + product(picked(k, zones[0]))).astype(BF16)
+        mine = placed(products, zones[1]) + own_term(k, everyone, zones[1])
+        part_ref[1] = mine
         if k < DEGREE:
-            level(k + 1, image(inner), inner)
+            snd_ref[k, 1] = mine.astype(BF16)
+        else:
+            esnd_ref[1] = part_ref[1, :, outer[1]].astype(BF16)
+        nearby(k + 1).start()
+        mine = placed(products, inner) + own_term(k, everyone, inner)
+        if k < DEGREE:
+            level(k + 1, mine, everyone, inner)
         else:
             filt_ref[...] = v_ref[k, :, rim : rim + nodes]
-            row_ref[b, rows : 2 * rows, rim : nodes - rim] = image(inner).astype(BF16)
+            row_ref[b, rows : 2 * rows, rim : nodes - rim] = mine.astype(BF16)
             send_around(1, 0)
         if k == DEGREE - 1:
             share(0)
 
+    def energy(side):
+        row_ref[b, rows : 2 * rows, lanes(edges[side], rim)] = (
+            part_ref[side, :, own[side]] + ercv_ref[side].astype(F32)
+        ).astype(BF16)
+
+    nearby(DEGREE + 1).wait_recv()
+    energy(1)
+    send_around(1, 1)
     pass_along(1, 0)
     pass_around(0, 0)
-    for f in flights[DEGREE + 1]:
-        f.wait_recv()
-    for side in (0, 1):
-        first = side * (nodes - rim)
-        own = slice(rim, zone) if side == 0 else slice(0, rim)
-        row_ref[b, rows : 2 * rows, first : first + rim] = (
-            part_ref[side, :, own] + ercv_ref[side].astype(F32)
-        ).astype(BF16)
-        send_around(1, 1 + side)
+    for g in range(GROUPS):
+        afar(DEGREE + 1, g).wait_recv()
+    energy(0)
+    send_around(1, 2)
     for part in (1, 2):
         pass_along(1, part)
         pass_around(0, part)
@@ -319,9 +371,10 @@
     inter_ref[...] = total[0:half, 0:rows]
     proj_ref[...] = jnp.concatenate([total[0:half, rows:], tail], axis=1)
 
-    for step in flights:
-        for f in step:
-            f.wait_send()
+    for step in range(DEGREE + 2):
+        nearby(step).wait_send()
+        for g in range(GROUPS):
+            afar(step, g).wait_send()
     for way in (0, 1):
         for hop in range(line - 1):
             for part in range(3):
@@ -367,6 +420,9 @@
             pltpu.VMEM((cells * local, ext), BF16),
             pltpu.VMEM((DEGREE + 1, rows, ext), BF16),
             pltpu.VMEM((rows, cells * local), F32),
+            pltpu.VMEM((1, ext), F32),
+            pltpu.VMEM((3, 2 * rim, cells * local), BF16),
+            pltpu.VMEM((rows, 2 * rim), F32),
             pltpu.VMEM((2, rows, 2 * rim), F32),
             pltpu.VMEM((DEGREE, 2, rows, 2 * rim), BF16),
             pltpu.VMEM((DEGREE, 2, rows, 2 * rim), BF16),
@@ -379,7 +435,8 @@
             pltpu.VMEM((line, wide, *packed), BF16),
             pltpu.VMEM((line, wide, *packed), BF16),
             pltpu.VMEM((chips, *packed), BF16),
-            dma((DEGREE + 2, 2)), dma((DEGREE + 2, 2)),
+            dma((DEGREE + 2, GROUPS)), dma((DEGREE + 2, GROUPS)),
+            dma((DEGREE + 2,)), dma((DEGREE + 2,)),
             dma((2, line, 3)), dma((line, 3)),
             dma((4, 2, 3)), dma((4, 2, 3)),
             dma((line,)), dma((line,)),

time: 92.6 us -> 87.5 us (0.945)
  the two profiles are of different devices: /device:TPU:88 before, /device:TPU:64 now
where the time goes in v4:
time: 87.5 us; the launch traced here: 87.3 us
  Pallas kernels  83.6 us (96%)
  local copies, waits for them, and re-layouts  2.98 us (3%)
    pallas_call x1, Pallas kernels, per_device(): pl.pallas_call(kernel, out_shape=(jax.ShapeDtypeStruct((rows, nodes), BF1...  83.6 us
    unnamed x7, local copies, waits for them, and re-layouts  2.98 us

profile of v4, /device:TPU:64, one launch (start us, length us, event | category | flops | bytes accessed | tf_op | source)
XLA Modules:
  0.0 87.3 jit_solution(9390450963630434701)
XLA Ops:
  0.6 83.6 %shard_map.67 = (bf16[96,1024]{1,0:T(8,128)(2,1)}, f32[48,96]{1,0:T(8,128)}, f32[48,96]{1,0:T(8,128)}) custom-call(bf16[96,1024]{1,0:T(8,128)(2,1)} %states_ref.1, bf16[2,512,512]{2,1,0:T(8,128)(2,1)} %cells_ref.1, s32[2,512]{1,0:T(2,128)} %conn_ref.1, f32[1,1024]{1,0:T(1,128)} %bitcast.5), custom_call_target="tpu_custom_call" | custom-call | tf_op jit(solution)/shard_map/pallas_call | solution.py:409
  84.3 0.0 copy-start.1
  84.3 1.6 %copy.10 = bf16[96,1024]{1,0:T(8,128)(2,1)} copy(bf16[96,1024]{1,0:T(8,128)(2,1)} %get-tuple-element.12) | data formatting | bytes 393216
  85.9 0.0 copy-done.1
  85.9 0.0 copy-start
  85.9 0.6 copy.11
  86.5 0.1 copy-done
  86.7 0.6 copy.12
Async XLA Ops:
  84.3 1.6 %copy-start.1 = (f32[48,96]{1,0:T(8,128)S(1)}, f32[48,96]{1,0:T(8,128)}, u32[]{:S(2)}) copy-start(f32[48,96]{1,0:T(8,128)} %get-tuple-element.7) | copy-start | bytes 55300
  85.9 0.7 copy-start

commit v5 on v4

--- a/solution.py
+++ b/solution.py
@@ -9,6 +9,7 @@
 DEGREE = 4
 WIDE = 4
 GROUPS = 3
+PIECES = 2
 STATE = ("state_0", "state_1")
 CENTER = 3.0
 HALF = 3.5
@@ -174,7 +175,10 @@
     near_ref[1, :, 0:zone] = itself.astype(BF16)
     near_ref[2, :, 0:zone] = (itself - near_ref[1, :, 0:zone].astype(F32)).astype(BF16)
 
-    parts = ((rim, nodes - zone), (edges[1], rim), (edges[0], rim))
+    piece = (nodes - zone) // PIECES
+    early = range(PIECES)
+    near, far = PIECES, PIECES + 1
+    parts = (*((rim + n * piece, piece) for n in early), (edges[1], rim), (edges[0], rim))
 
     def along(way, block, part):
         block = lax.rem(block + line, line)
@@ -244,9 +248,13 @@
         if k:
             level(k, part_ref[1] + rcv_ref[k - 1, 1].astype(F32), everyone, zones[1])
         if k == DEGREE:
-            share(1)
+            share(near)
         acc_ref[...] += product(picked(k, zones[1]))
         base_ref[...] = placed(acc_ref[...].astype(BF16), zones[0])
+        if k == DEGREE:
+            for part in early:
+                pass_along(1, part)
+                pass_around(0, part)
         for g, group in enumerate(groups):
             afar(k, g).wait_recv()
             if k:
@@ -262,7 +270,7 @@
                 esnd_ref[0, group, :] = part_ref[0, group, outer[0]].astype(BF16)
             afar(k + 1, g).start()
         if k == DEGREE:
-            share(2)
+            share(far)
         products = (acc_ref[...] + product(picked(k, zones[0]))).astype(BF16)
         mine = placed(products, zones[1]) + own_term(k, everyone, zones[1])
         part_ref[1] = mine
@@ -277,9 +285,11 @@
         else:
             filt_ref[...] = v_ref[k, :, rim : rim + nodes]
             row_ref[b, rows : 2 * rows, rim : nodes - rim] = mine.astype(BF16)
-            send_around(1, 0)
+            for part in early:
+                send_around(1, part)
         if k == DEGREE - 1:
-            share(0)
+            for part in early:
+                share(part)
 
     def energy(side):
         row_ref[b, rows : 2 * rows, lanes(edges[side], rim)] = (
@@ -288,23 +298,28 @@
 
     nearby(DEGREE + 1).wait_recv()
     energy(1)
-    send_around(1, 1)
-    pass_along(1, 0)
-    pass_around(0, 0)
+    send_around(1, near)
+    pass_along(1, near)
+    pass_around(0, near)
+    for part in early:
+        pass_along(2, part)
+    pass_along(1, far)
+    pass_around(0, far)
+    for part in early:
+        pass_around(1, part)
+    pass_along(2, near)
+    pass_around(1, near)
+    pass_along(2, far)
     for g in range(GROUPS):
         afar(DEGREE + 1, g).wait_recv()
     energy(0)
-    send_around(1, 2)
-    for part in (1, 2):
-        pass_along(1, part)
-        pass_around(0, part)
-    for hop in range(2, max(line, 3)):
-        for part in range(3):
+    send_around(1, far)
+    pass_around(1, far)
+    for hop in range(3, line):
+        for part in range(len(parts)):
             pass_along(hop, part)
-            if hop == 2:
-                pass_around(1, part)
     for kind in (0, 1):
-        for part in range(3):
+        for part in range(len(parts)):
             for turn in (2, 3):
                 arrive(turn, kind, part)
 
@@ -377,7 +392,7 @@
             afar(step, g).wait_send()
     for way in (0, 1):
         for hop in range(line - 1):
-            for part in range(3):
+            for part in range(len(parts)):
 
                 @pl.when(goes(way, hop))
                 def _():
@@ -385,7 +400,7 @@
 
     for turn in range(4):
         for kind in (0, 1):
-            for part in range(3):
+            for part in range(len(parts)):
                 around(turn, kind, part).wait_send()
     for i in range(line):
         to_sibling(i).wait_send()
@@ -437,8 +452,8 @@
             pltpu.VMEM((chips, *packed), BF16),
             dma((DEGREE + 2, GROUPS)), dma((DEGREE + 2, GROUPS)),
             dma((DEGREE + 2,)), dma((DEGREE + 2,)),
-            dma((2, line, 3)), dma((line, 3)),
-            dma((4, 2, 3)), dma((4, 2, 3)),
+            dma((2, line, PIECES + 2)), dma((line, PIECES + 2)),
+            dma((4, 2, PIECES + 2)), dma((4, 2, PIECES + 2)),
             dma((line,)), dma((line,)),
             dma((line, wide)), dma((chips,)),
         ],

time: 87.5 us -> 92.7 us (1.059)
  Pallas kernels: 83.6 us -> 88.9 us
    pallas_call x1, Pallas kernels: 83.6 us -> 88.9 us  [per_device(): pl.pallas_call(kernel, out_shape=(jax.ShapeDtypeStruct((rows, nodes), BF1...]
where the time goes in v5:
time: 92.7 us; the launch traced here: 92.5 us
  Pallas kernels  88.9 us (96%)
  local copies, waits for them, and re-layouts  2.98 us (3%)
    pallas_call x1, Pallas kernels, per_device(): pl.pallas_call(kernel, out_shape=(jax.ShapeDtypeStruct((rows, nodes), BF1...  88.9 us
    unnamed x7, local copies, waits for them, and re-layouts  2.98 us

profile of v5, /device:TPU:64, one launch (start us, length us, event | category | flops | bytes accessed | tf_op | source)
XLA Modules:
  0.0 92.5 jit_solution(8489789999734895353)
XLA Ops:
  0.6 88.9 %shard_map.67 = (bf16[96,1024]{1,0:T(8,128)(2,1)}, f32[48,96]{1,0:T(8,128)}, f32[48,96]{1,0:T(8,128)}) custom-call(bf16[96,1024]{1,0:T(8,128)(2,1)} %states_ref.1, bf16[2,512,512]{2,1,0:T(8,128)(2,1)} %cells_ref.1, s32[2,512]{1,0:T(2,128)} %conn_ref.1, f32[1,1024]{1,0:T(1,128)} %bitcast.5), custom_call_target="tpu_custom_call" | custom-call | tf_op jit(solution)/shard_map/pallas_call | solution.py:424
  89.5 0.0 copy-start.1
  89.5 1.6 %copy.10 = bf16[96,1024]{1,0:T(8,128)(2,1)} copy(bf16[96,1024]{1,0:T(8,128)(2,1)} %get-tuple-element.12) | data formatting | bytes 393216
  91.2 0.0 copy-done.1
  91.2 0.0 copy-start
  91.2 0.6 copy.11
  91.8 0.1 copy-done
  91.9 0.6 copy.12
Async XLA Ops:
  89.5 1.6 %copy-start.1 = (f32[48,96]{1,0:T(8,128)S(1)}, f32[48,96]{1,0:T(8,128)}, u32[]{:S(2)}) copy-start(f32[48,96]{1,0:T(8,128)} %get-tuple-element.7) | copy-start | bytes 55300
  91.2 0.7 copy-start

commit v6 on v5

--- a/solution.py
+++ b/solution.py
@@ -251,10 +251,6 @@
             share(near)
         acc_ref[...] += product(picked(k, zones[1]))
         base_ref[...] = placed(acc_ref[...].astype(BF16), zones[0])
-        if k == DEGREE:
-            for part in early:
-                pass_along(1, part)
-                pass_around(0, part)
         for g, group in enumerate(groups):
             afar(k, g).wait_recv()
             if k:
@@ -299,25 +295,21 @@
     nearby(DEGREE + 1).wait_recv()
     energy(1)
     send_around(1, near)
-    pass_along(1, near)
-    pass_around(0, near)
     for part in early:
-        pass_along(2, part)
-    pass_along(1, far)
-    pass_around(0, far)
-    for part in early:
-        pass_around(1, part)
-    pass_along(2, near)
-    pass_around(1, near)
-    pass_along(2, far)
+        pass_along(1, part)
+        pass_around(0, part)
     for g in range(GROUPS):
         afar(DEGREE + 1, g).wait_recv()
     energy(0)
     send_around(1, far)
-    pass_around(1, far)
-    for hop in range(3, line):
+    for part in (near, far):
+        pass_along(1, part)
+        pass_around(0, part)
+    for hop in range(2, max(line, 3)):
         for part in range(len(parts)):
             pass_along(hop, part)
+            if hop == 2:
+                pass_around(1, part)
     for kind in (0, 1):
         for part in range(len(parts)):
             for turn in (2, 3):

time: 92.7 us -> 88.8 us (0.958)
  the two profiles are of different devices: /device:TPU:64 before, /device:TPU:14 now
where the time goes in v6:
time: 88.8 us; the launch traced here: 88.5 us
  Pallas kernels  84.9 us (96%)
  local copies, waits for them, and re-layouts  2.98 us (3%)
    pallas_call x1, Pallas kernels, per_device(): pl.pallas_call(kernel, out_shape=(jax.ShapeDtypeStruct((rows, nodes), BF1...  84.9 us
    unnamed x7, local copies, waits for them, and re-layouts  2.98 us

profile of v6, /device:TPU:14, one launch (start us, length us, event | category | flops | bytes accessed | tf_op | source)
XLA Modules:
  0.0 88.5 jit_solution(17709629685119652705)
XLA Ops:
  0.6 84.9 %shard_map.67 = (bf16[96,1024]{1,0:T(8,128)(2,1)}, f32[48,96]{1,0:T(8,128)}, f32[48,96]{1,0:T(8,128)}) custom-call(bf16[96,1024]{1,0:T(8,128)(2,1)} %states_ref.1, bf16[2,512,512]{2,1,0:T(8,128)(2,1)} %cells_ref.1, s32[2,512]{1,0:T(2,128)} %conn_ref.1, f32[1,1024]{1,0:T(1,128)} %bitcast.5), custom_call_target="tpu_custom_call" | custom-call | tf_op jit(solution)/shard_map/pallas_call | solution.py:416
  85.5 0.0 copy-start.1
  85.5 1.6 %copy.10 = bf16[96,1024]{1,0:T(8,128)(2,1)} copy(bf16[96,1024]{1,0:T(8,128)(2,1)} %get-tuple-element.12) | data formatting | bytes 393216
  87.2 0.0 copy-done.1
  87.2 0.0 copy-start
  87.2 0.6 copy.11
  87.8 0.1 copy-done
  87.9 0.6 copy.12
Async XLA Ops:
  85.5 1.6 %copy-start.1 = (f32[48,96]{1,0:T(8,128)S(1)}, f32[48,96]{1,0:T(8,128)}, u32[]{:S(2)}) copy-start(f32[48,96]{1,0:T(8,128)} %get-tuple-element.7) | copy-start | bytes 55300
  87.2 0.7 copy-start
